TPU v7x, 32 devices: a whole 2x2x4 slice. The times are simulated.
32 devices in a mesh: fault: 16 (over z, y, core), off: 2 (over x).
Axes of the slice: x: 2, y: 2, z: 4, core: 2. Of those that a mesh axis runs over, the one named last changes fastest.
Arguments:
- modal_state: float32 [9, 56, 1024], P(None, None, ('fault', 'off')), may hold values from -6 to 6
- star_mats: float32 [3, 9, 9, 1024], P(None, None, None, ('fault', 'off')), may hold values from -2 to 2
- flux_local: float32 [4, 9, 9, 1024], P(None, None, None, ('fault', 'off')), may hold values from -1 to 1
- flux_nbr: float32 [4, 9, 9, 1024], P(None, None, None, ('fault', 'off')), may hold values from -1 to 1
- stiff_time: float32 [3, 56, 56], replicated, may hold values from -0.75 to 0.75
- stiff_vol: float32 [3, 56, 56], replicated, may hold values from -0.375 to 0.375
- flux_minus: float32 [4, 56, 56], replicated, may hold values from -0.375 to 0.375
- face_proj: float32 [4, 56, 21], replicated, may hold values from -0.75 to 0.75
- face_turn: float32 [3, 21, 21], replicated, may hold values from -1.25 to 1.25
- face_lift: float32 [4, 21, 56], replicated, may hold values from -0.625 to 0.625
- cluster: int32 [1024], P(('fault', 'off')), may hold values from 0 to 1, as said below
- send_elem: int32 [16, 2, 52], P('fault', 'off'), may hold values from 0 to 31
- send_face: int32 [16, 2, 52], P('fault', 'off'), may hold values from 0 to 3
- nbr_index: int32 [4, 1024], P(None, ('fault', 'off')), may hold values from 0 to 179, as said below
- orientation: int32 [4, 1024], P(None, ('fault', 'off')), may hold values from 0 to 2
- source_elem: int32 [16], replicated, may hold values from 0 to 1023
- source_term: float32 [16, 9, 56], replicated, may hold values from -6 to 6
Outputs:
- new_state: float32 [9, 56, 1024], P(None, None, ('fault', 'off'))
Inputs may be any that keep to these rules, and one draw needn't show every extreme that they name: `cluster`: each device holds at most 16 fine elements, and some device exactly 16 in every draw. `nbr_index`: on each device, entries below 128 name the device's own face traces; every received entry 128 .. 179 is named by exactly one face of the device.
All inputs are finite; a program needn't handle non-finite values.
Results may differ from a plain program's by a relative error of at most 0.0003.
Values sent between devices are 32-bit elements; how exact they have to be, the bound alone decides.
No kernel may reach another device: no remote copies, remote signals or barrier semaphores. Data moves between devices by JAX's collectives and lax.ppermute only.
A program may use at most 64 MiB of HBM per device.

v0:
```python
import functools
import math

import jax
import jax.numpy as jnp
from jax import lax
from jax.experimental import pallas as pl
from jax.experimental.pallas import tpu as pltpu
from jax.sharding import PartitionSpec as P

Q = 9
M = 56
J = 21
JP = 24
E = 32
LANES = 128
W = 384
SF = 16
SO = 10
SRC = 16
TERMS = 6
EARLY = [0.5 ** (k + 1) / math.factorial(k + 1) for k in range(TERMS)]
LATE = [(1.0 - 0.5 ** (k + 1)) / math.factorial(k + 1) for k in range(TERMS)]
F32 = jnp.float32
BF16 = jnp.bfloat16
TAB = 256


def lane_iota(rows, width=LANES):
    return lax.broadcasted_iota(jnp.int32, (rows, width), 1)


def row_iota(rows, width=LANES):
    return lax.broadcasted_iota(jnp.int32, (rows, width), 0)


def halves(rows):
    lane = lane_iota(rows)
    return lane < 64, (lane & 32) == 0


def roll(x, shift):
    return pltpu.roll(x, shift, 1)


def split(x):
    high = x.astype(BF16)
    low = (x - high.astype(F32)).astype(BF16)
    return high, low


def dot(a, b):
    return lax.dot_general(a, b, (((1,), (0,)), ((), ())), preferred_element_type=F32)


def dot_nt(a, b):
    return lax.dot_general(a, b, (((1,), (1,)), ((), ())), preferred_element_type=F32)


def product(left, right):
    high, low = split(right)
    rows = left.shape[0] // 2
    width = right.shape[1]
    wide = dot(left, jnp.concatenate([high, low], axis=1))
    return wide[:rows, :width] + (wide[rows:, :width] + wide[:rows, width:])


def stack_split(x):
    high, low = split(x)
    return jnp.concatenate([high.astype(F32), low.astype(F32)], axis=0).astype(BF16)


def spread(columns):
    first, even = halves(8)
    tiles = []
    for column in columns[:2]:
        turned = roll(column, 64)
        for pair in (jnp.where(first, column, turned), jnp.where(first, turned, column)):
            moved = roll(pair, 32)
            tiles.append(jnp.where(even, pair, moved))
            tiles.append(jnp.where(even, moved, pair))
    pair = jnp.where(first, columns[2], roll(columns[2], 64))
    tiles.append(jnp.where(even, pair, roll(pair, 32)))
    return tiles


def group_swap(parts):
    first, even = halves(8)
    a0, a1, a2, a3 = parts
    out = []
    p = [jnp.where(first, a0, roll(a2, 64)), jnp.where(first, a1, roll(a3, 64))]
    r = [jnp.where(first, roll(a0, 64), a2), jnp.where(first, roll(a1, 64), a3)]
    for x, y in (p, r):
        out.append(jnp.where(even, x, roll(y, 32)))
        out.append(jnp.where(even, roll(x, 96), y))
    return out


def group_place(parts):
    total = parts[0]
    for group, part in enumerate(parts[1:], 1):
        total = total + roll(part, 32 * group)
    return total


def widen(x, pad):
    rows = x.shape[0]
    pad[0:rows, 0:E] = x
    return pad[0:rows, :]


def weigh(rows_of, x_ref, y_ref, count):
    for tile in range(M // 8):
        spans = spread([x_ref[tile * 8 : tile * 8 + 8, c * 128 : c * 128 + 128] for c in range(3)])
        for d in range(count):
            for c in range(3):
                total = rows_of[d * 16 : d * 16 + 1, c * 128 : c * 128 + 128] * spans[0]
                for p in range(1, Q):
                    total = total + rows_of[d * 16 + p : d * 16 + p + 1, c * 128 : c * 128 + 128] * spans[p]
                start = d * M + tile * 8
                y_ref[start : start + 8, c * 128 : c * 128 + 128] = total


def predict(star, left, x_ref, y_ref, first_ref, second_ref):
    y_ref[3 * M : 3 * M + 8, :] = jnp.zeros((8, W), F32)
    state = x_ref[...]
    first_ref[...] = EARLY[0] * state
    if second_ref is not None:
        second_ref[...] = LATE[0] * state

    def step(k, carry):
        weigh(star, x_ref, y_ref, 3)
        result = product(left[...], y_ref[0 : 3 * M + 8, :])
        x_ref[...] = result
        early = jnp.float32(EARLY[1])
        late = jnp.float32(LATE[1])
        for degree in range(2, TERMS):
            early = jnp.where(k == degree, EARLY[degree], early)
            late = jnp.where(k == degree, LATE[degree], late)
        first_ref[...] = first_ref[...] + early * result
        if second_ref is not None:
            second_ref[...] = second_ref[...] + late * result
        return carry

    lax.fori_loop(1, TERMS, step, 0)


def make_table(project, x, tab_ref):
    faced = product(project, x)
    for tile in range(3):
        for c in range(3):
            parts = [
                faced[f * JP + tile * 8 : f * JP + tile * 8 + 8, c * 128 : c * 128 + 128] for f in range(4)
            ]
            swapped = group_swap(parts)
            for g in range(4 if c < 2 else 1):
                row = (c * 4 + g) * JP + tile * 8
                tab_ref[row : row + 8, :] = swapped[g]
    tab_ref[Q * JP : TAB, :] = jnp.zeros((TAB - Q * JP, LANES), F32)


def send_rows(pick, tab_ref):
    high, low = split(tab_ref[...])
    return dot_nt(pick, high) + dot_nt(pick, low)


def off_rank():
    return lax.axis_index("off")


def put_sends(rows, bw_ref, fw_ref, self_ref, off_refs):
    bw_ref[...] = rows[0:16]
    fw_ref[...] = rows[16:32]
    self_ref[...] = rows[32:48]
    for k, ref in enumerate(off_refs):
        ref[...] = rows[48 + 16 * k : 64 + 16 * k]


def first_kernel(n_off, state_in, star_in, stiff_in, proj_in, elem_in, face_in, *refs):
    (state_out, first_out, second_out, star_out, left_out, proj_out, tab_out, pick_out, bw, fw, own) = refs[:11]
    offs = refs[11 : 11 + n_off - 1]
    x_ref, y_ref, pad, high_pad, slot_pad = refs[11 + n_off - 1 :]
    pad[...] = jnp.zeros((64, LANES), F32)
    for c in range(3):
        parts = [widen(state_in[q], pad) for q in range(4 * c, min(4 * c + 4, Q))]
        column = group_place(parts)
        x_ref[:, c * 128 : c * 128 + 128] = column
        state_out[:, c * 128 : c * 128 + 128] = column
    pad[...] = jnp.zeros((64, LANES), F32)
    for d in range(3):
        for c in range(3):
            parts = []
            for q in range(4 * c, min(4 * c + 4, Q)):
                pad[0:Q, 0:E] = star_in[d, q]
                parts.append(pad[0:16, :])
            star_out[d * 16 : d * 16 + 16, c * 128 : c * 128 + 128] = group_place(parts)
    high_pad[...] = jnp.zeros((256, LANES), F32)
    for d in range(3):
        high_pad[d * M : d * M + M, 0:M] = stiff_in[d]
    left_out[...] = stack_split(high_pad[...].T[0:M, 0 : 3 * M + 8])
    high_pad[...] = jnp.zeros((256, LANES), F32)
    for f in range(4):
        high_pad[f * 64 : f * 64 + M, 0:J] = proj_in[f]
    turned = high_pad[...].T
    proj_out[...] = stack_split(
        jnp.concatenate([turned[0:JP, f * 64 : f * 64 + M] for f in range(4)], axis=0)
    )
    slots = elem_in.shape[2]
    slot_pad[...] = jnp.zeros((8, LANES), jnp.int32)
    slot_pad[0:1, 0:slots] = face_in[0] * E + elem_in[0] + 1
    rows = 32 + 16 * n_off
    row = row_iota(rows)
    block = row >> 4
    within = row & 15
    target = lax.rem(block - 2 + off_rank(), n_off)
    slot = jnp.where(row < 32, row, jnp.where(within < SO, 32 + target * SO + within, -1))
    wanted = jnp.where(lane_iota(rows) == slot, slot_pad[0:1, :], 0)
    entry = jnp.sum(wanted.astype(F32), axis=1, keepdims=True)
    pick = jnp.where(lane_iota(rows).astype(F32) + 1.0 == entry, 1.0, 0.0).astype(BF16)
    pick_out[...] = pick

    predict(star_out, left_out, x_ref, y_ref, first_out, second_out)
    make_table(proj_out[...], first_out[...], tab_out)
    put_sends(send_rows(pick, tab_out), bw, fw, own, offs)


def gather_local(pick, tab_ref):
    high, low = split(tab_ref[0 : Q * JP + 8, :])
    return dot(high, pick) + dot(low, pick)


def side_kernel(
    n_off,
    first_in,
    star,
    tab,
    local_in,
    nbr_in,
    vol_in,
    minus_in,
    turn_in,
    lift_in,
    index_in,
    orient_in,
    cluster_in,
    source_elem,
    source_in,
    part_out,
    coef_out,
    fnbr_out,
    left_out,
    lift_out,
    here_out,
    pick_here_out,
    pick_far_out,
    flags_out,
    source_out,
    y_ref,
    pad,
    tall,
    turn_pad,
    lift_pad,
    ipad,
):
    pad[...] = jnp.zeros((64, LANES), F32)
    for d in range(3):
        coef_out[d * 16 : d * 16 + 16, :] = star[d * 16 : d * 16 + 16, :]
    for f in range(4):
        for c in range(3):
            parts = []
            for q in range(4 * c, min(4 * c + 4, Q)):
                pad[0:Q, 0:E] = local_in[f, q]
                parts.append(pad[0:16, :])
            coef_out[(3 + f) * 16 : (4 + f) * 16, c * 128 : c * 128 + 128] = group_place(parts)
    for q in range(Q):
        parts = []
        for f in range(4):
            pad[0:Q, 0:E] = nbr_in[f, q]
            parts.append(pad[0:16, :])
        fnbr_out[q * 16 : q * 16 + 16, :] = group_place(parts)
    tall[...] = jnp.zeros((512, LANES), F32)
    for d in range(3):
        tall[d * M : d * M + M, 0:M] = vol_in[d]
    for f in range(4):
        tall[(3 + f) * M : (4 + f) * M, 0:M] = minus_in[f]
    left_out[...] = stack_split(tall[...].T[0:M, 0 : 7 * M + 8])
    turn_pad[...] = jnp.zeros((3 * JP, LANES), F32)
    for o in range(3):
        turn_pad[o * JP : o * JP + J, 0:J] = turn_in[o]
    tall[...] = jnp.zeros((512, LANES), F32)
    lift_pad[...] = jnp.zeros((LANES, LANES), F32)
    for f in range(4):
        lift_pad[0:J, 0:M] = lift_in[f]
        tall[f * 3 * JP : (f + 1) * 3 * JP, :] = lax.dot_general(
            turn_pad[...],
            lift_pad[...],
            (((1,), (0,)), ((), ())),
            precision=lax.Precision.HIGHEST,
            preferred_element_type=F32,
        )
    lift_out[...] = stack_split(tall[...].T[0:M, 0 : 12 * JP])
    ipad[...] = jnp.zeros((8, LANES), jnp.int32)
    ipad[0:4, 0:E] = index_in[...]
    index_row = group_place([ipad[f : f + 1, :] for f in range(4)])
    ipad[0:4, 0:E] = orient_in[...]
    ipad[4:5, 0:E] = cluster_in[...]
    orient = ipad[...]
    twice = orient + roll(orient, 64)
    flags_out[...] = twice + roll(twice, 32)
    pick_here = jnp.where(row_iota(LANES) == index_row, 1.0, 0.0).astype(BF16)
    pick_here_out[...] = pick_here
    rows = 32 + 16 * n_off
    row = row_iota(rows)
    within = row & 15
    source = lax.rem(off_rank() + n_off + 2 - (row >> 4), n_off)
    place = jnp.where(
        row < 32, LANES + row, jnp.where(within < SO, LANES + 32 + source * SO + within, -1)
    )
    pick_far_out[...] = jnp.where(place == index_row, 1.0, 0.0).astype(BF16)
    here_out[...] = gather_local(pick_here, tab)
    tall[...] = jnp.zeros((512, LANES), F32)
    for s in range(SRC):
        tall[s * 16 : s * 16 + Q, 0:M] = source_in[s]
    origin = (lax.axis_index("fault") * n_off + off_rank()) * E
    row16 = row_iota(16, W)
    lane16 = lane_iota(16, W)
    for s in range(SRC):
        spot = source_elem[s] - origin
        inside = jnp.logical_and(spot >= 0, spot < E)
        goal = jnp.where(inside, spot, -100000)
        y_ref[s * 16 : s * 16 + 16, :] = jnp.where(
            jnp.logical_and(lane16 == row16 * E + goal, row16 < Q), 1.0, 0.0
        )
    picks = y_ref[0 : SRC * 16, :].astype(BF16)
    high, low = split(tall[...].T[0:M, 0 : SRC * 16])
    rest = tall[...].T[0:M, 0 : SRC * 16] - high.astype(F32) - low.astype(F32)
    source_out[...] = dot(high, picks) + (dot(low, picks) + dot(rest.astype(BF16), picks))

    weigh(coef_out, first_in, y_ref, 7)
    y_ref[7 * M : 7 * M + 8, :] = jnp.zeros((8, W), F32)
    part_out[...] = product(left_out[...], y_ref[...])


def arrive(n_off, fw, bw, own, offs, pick_far, stage):
    stage[0:16, :] = fw[...]
    stage[16:32, :] = bw[...]
    stage[32:48, :] = own[...]
    for k, ref in enumerate(offs):
        stage[48 + 16 * k : 64 + 16 * k, :] = ref[...]
    turned = stage[...].T[0 : Q * JP + 8, :]
    high, low = split(turned)
    return dot(high, pick_far[...]) + dot(low, pick_far[...])


def neighbour_flux(near_ref, fnbr, flags, lift, y_ref):
    for tile in range(3):
        near = [near_ref[p * JP + tile * 8 : p * JP + tile * 8 + 8, :] for p in range(Q)]
        fluxes = []
        for q in range(Q):
            total = fnbr[q * 16 : q * 16 + 1, :] * near[0]
            for p in range(1, Q):
                total = total + fnbr[q * 16 + p : q * 16 + p + 1, :] * near[p]
            fluxes.append(total)
        zero = jnp.zeros((8, LANES), F32)
        for c in range(3):
            parts = [fluxes[4 * c + g] if 4 * c + g < Q else zero for g in range(4)]
            swapped = group_swap(parts)
            for f in range(4):
                facing = flags[f : f + 1, :]
                for o in range(3):
                    start = (f * 3 + o) * JP + tile * 8
                    y_ref[start : start + 8, c * 128 : c * 128 + 128] = jnp.where(
                        facing == o, swapped[f], 0.0
                    )
    return product(lift[...], y_ref[0 : 12 * JP, :])


def wide_fine(flags):
    row = flags[4:5, :] == 1
    return row


def middle_kernel(
    n_off, state, second, part, here, fnbr, flags, lift, star, left, proj, pick, pick_far, own, fw, bw, *refs
):
    offs = refs[: n_off - 1]
    outs = refs[n_off - 1 :]
    near_out, half_out, later_out, tab_out, bw_out, fw_out, own_out = outs[:7]
    off_outs = outs[7 : 7 + n_off - 1]
    x_ref, y_ref, stage, acc = outs[7 + n_off - 1 :]
    near_out[...] = here[...] + arrive(n_off, fw, bw, own, offs, pick_far, stage)
    total = part[...] + neighbour_flux(near_out, fnbr, flags, lift, y_ref)
    fine = jnp.concatenate([wide_fine(flags)] * 3, axis=1)
    base = state[...]
    half = jnp.where(fine, base + total, base)
    half_out[...] = half
    x_ref[...] = half
    predict(star, left, x_ref, y_ref, acc, None)
    later = jnp.where(fine, acc[...], second[...])
    later_out[...] = later
    make_table(proj[...], later, tab_out)
    put_sends(send_rows(pick[...], tab_out), bw_out, fw_out, own_out, off_outs)


def late_side_kernel(
    first, second, later, half, source, near_first, tab, coef, left, flags, pick_here, base_out, here_out, x_ref, y_ref
):
    row = wide_fine(flags)
    fine = jnp.concatenate([row] * 3, axis=1)
    x_ref[...] = jnp.where(fine, later[...], first[...] + second[...])
    weigh(coef, x_ref, y_ref, 7)
    y_ref[7 * M : 7 * M + 8, :] = jnp.zeros((8, W), F32)
    base_out[...] = half[...] + source[...] + product(left[...], y_ref[...])
    here_out[...] = gather_local(pick_here[...], tab) + jnp.where(row, 0.0, near_first[...])


def last_kernel(n_off, base, here, fnbr, flags, lift, pick_far, own, fw, bw, *refs):
    offs = refs[: n_off - 1]
    out, near, y_ref, stage = refs[n_off - 1 :]
    near[...] = here[...] + arrive(n_off, fw, bw, own, offs, pick_far, stage)
    total = base[...] + neighbour_flux(near, fnbr, flags, lift, y_ref)
    for q in range(Q):
        column = total[:, (q // 4) * 128 : (q // 4) * 128 + 128]
        if q % 4:
            column = roll(column, 128 - 32 * (q % 4))
        out[q] = column[:, 0:E]


def shape(*dims, dtype=F32):
    return jax.ShapeDtypeStruct(dims, dtype)


def call(kernel, ins, outs, scratch, name, smem=(), cost=2000000):
    specs = [
        pl.BlockSpec(memory_space=pltpu.SMEM if k in smem else pltpu.VMEM) for k in range(len(ins))
    ]
    return pl.pallas_call(
        kernel,
        in_specs=specs,
        out_specs=[pl.BlockSpec(memory_space=pltpu.VMEM)] * len(outs),
        out_shape=outs,
        scratch_shapes=scratch,
        name=name,
        compiler_params=pltpu.CompilerParams(vmem_limit_bytes=16 * 1024 * 1024),
        cost_estimate=pl.CostEstimate(flops=cost * 1000, bytes_accessed=cost, transcendentals=0),
    )(*ins)


def trade(bw, fw, offs, n_fault, n_off):
    up = [(i, (i + 1) % n_fault) for i in range(n_fault)]
    down = [((i + 1) % n_fault, i) for i in range(n_fault)]
    got = []
    for k, rows in enumerate(offs, 1):
        got.append(lax.ppermute(rows, "off", [(j, (j + k) % n_off) for j in range(n_off)]))
    return lax.ppermute(fw, "fault", up), lax.ppermute(bw, "fault", down), got


def on_device(
    n_fault,
    n_off,
    modal_state,
    star_mats,
    flux_local,
    flux_nbr,
    stiff_time,
    stiff_vol,
    flux_minus,
    face_proj,
    face_turn,
    face_lift,
    cluster,
    send_elem,
    send_face,
    nbr_index,
    orientation,
    source_elem,
    source_term,
):
    vmem = pltpu.VMEM
    rows = 32 + 16 * n_off
    wide = shape(M, W)
    table = shape(TAB, LANES)
    block = shape(16, TAB)
    near = shape(Q * JP + 8, LANES)
    outs = call(
        functools.partial(first_kernel, n_off),
        (modal_state, star_mats, stiff_time, face_proj, send_elem, send_face),
        [
            wide,
            wide,
            wide,
            shape(48, W),
            shape(2 * M, 3 * M + 8, dtype=BF16),
            shape(8 * JP, M, dtype=BF16),
            table,
            shape(rows, LANES, dtype=BF16),
        ]
        + [block] * (3 + n_off - 1),
        [
            vmem((M, W), F32),
            vmem((3 * M + 8, W), F32),
            vmem((64, LANES), F32),
            vmem((256, LANES), F32),
            vmem((8, LANES), jnp.int32),
        ],
        "first",
    )
    state, first, second, star, left, proj, tab, pick, bw, fw, own = outs[:11]
    got_fw, got_bw, got_off = trade(bw, fw, outs[11:], n_fault, n_off)
    part, coef, fnbr, left_all, lift, here, pick_here, pick_far, flags, source = call(
        functools.partial(side_kernel, n_off),
        (
            first,
            star,
            tab,
            flux_local,
            flux_nbr,
            stiff_vol,
            flux_minus,
            face_turn,
            face_lift,
            nbr_index,
            orientation,
            cluster.reshape(1, E),
            source_elem,
            source_term,
        ),
        [
            wide,
            shape(7 * 16, W),
            shape(Q * 16, LANES),
            shape(2 * M, 7 * M + 8, dtype=BF16),
            shape(2 * M, 12 * JP, dtype=BF16),
            near,
            shape(LANES, LANES, dtype=BF16),
            shape(rows, LANES, dtype=BF16),
            shape(8, LANES, dtype=jnp.int32),
            wide,
        ],
        [
            vmem((7 * M + 8, W), F32),
            vmem((64, LANES), F32),
            vmem((512, LANES), F32),
            vmem((3 * JP, LANES), F32),
            vmem((LANES, LANES), F32),
            vmem((8, LANES), jnp.int32),
        ],
        "side",
        smem=(12,),
    )
    outs = call(
        functools.partial(middle_kernel, n_off),
        (state, second, part, here, fnbr, flags, lift, star, left, proj, pick, pick_far, own, got_fw, got_bw, *got_off),
        [near, wide, wide, table] + [block] * (3 + n_off - 1),
        [vmem((M, W), F32), vmem((12 * JP, W), F32), vmem((rows, TAB), F32), vmem((M, W), F32)],
        "middle",
    )
    near_first, half, later, tab, bw, fw, own = outs[:7]
    got_fw, got_bw, got_off = trade(bw, fw, outs[7:], n_fault, n_off)
    base, here = call(
        late_side_kernel,
        (first, second, later, half, source, near_first, tab, coef, left_all, flags, pick_here),
        [wide, near],
        [vmem((M, W), F32), vmem((7 * M + 8, W), F32)],
        "late_side",
    )
    (result,) = call(
        functools.partial(last_kernel, n_off),
        (base, here, fnbr, flags, lift, pick_far, own, got_fw, got_bw, *got_off),
        [shape(Q, M, E)],
        [vmem((Q * JP + 8, LANES), F32), vmem((12 * JP, W), F32), vmem((rows, TAB), F32)],
        "last",
    )
    return result


def solution(mesh):
    n_fault, n_off = mesh.shape["fault"], mesh.shape["off"]
    both = ("fault", "off")
    in_specs = (
        P(None, None, both),
        P(None, None, None, both),
        P(None, None, None, both),
        P(None, None, None, both),
        P(),
        P(),
        P(),
        P(),
        P(),
        P(),
        P(both),
        P("fault", "off", None),
        P("fault", "off", None),
        P(None, both),
        P(None, both),
        P(),
        P(),
    )
    return jax.shard_map(
        functools.partial(on_device, n_fault, n_off),
        mesh=mesh,
        in_specs=in_specs,
        out_specs=P(None, None, both),
        check_vma=False,
    )
```

profile of v0, /device:TPU:0, one launch (start us, length us, event | category | flops | bytes accessed | tf_op | source)
XLA Modules:
  0.0 31.1 jit_solution(5475357810236264858)
XLA Ops:
  0.0 0.9 %copy.20.proj_in = f32[4,56,21]{2,1,0:T(8,128)S(1)} copy(f32[4,56,21]{1,0,2:T(4,128)} %param.24) | data formatting | bytes 37632 | tf_op args[7]
  0.9 0.0 copy-start.12
  0.9 1.0 %copy.19.star_in = f32[3,9,9,32]{3,2,1,0:T(8,128)S(1)} copy(f32[3,9,9,32]{3,0,2,1:T(4,128)} %param.18) | data formatting | bytes 62208 | tf_op args[1]
  1.9 0.0 copy-done.12
  1.9 0.0 copy-start.1
  1.9 0.0 copy-start.6
  1.9 0.0 copy-start.7
  1.9 0.1 copy.18.state_in
  2.1 0.7 %copy-done.1 = f32[3,56,56]{2,1,0:T(8,128)S(1)} copy-done((f32[3,56,56]{2,1,0:T(8,128)S(1)}, f32[3,56,56]{2,1,0:T(8,128)}, u32[]{:S(2)}) %copy-start.1) | copy-done | bytes 37656
  2.8 0.0 copy-done.6
  2.8 0.0 copy-done.7
  2.8 0.0 copy-start.14
  2.8 0.0 copy-start.13
  2.8 3.5 %first.1 = (f32[56,384]{1,0:T(8,128)S(1)}, f32[56,384]{1,0:T(8,128)S(1)}, f32[56,384]{1,0:T(8,128)S(1)}, f32[48,384]{1,0:T(8,128)S(1)}, bf16[112,176]{1,0:T(8,12...) custom-call(f32[9,56,32]{2,1,0:T(8,128)S(1)} %copy.18.state_in, ...), custom_call_target="tpu_custom_call" | custom-call | flops 2000000000 | bytes 2000000 | tf_op jit(solution)/shard_map/first/pallas_call | solution.py:437
  6.3 0.0 copy-start.10
  6.3 0.5 %collective-permute-start = (f32[16,256]{1,0:T(8,128)S(1)}, f32[16,256]{1,0:T(8,128)S(1)}, u32[]{:S(2)}, u32[]{:S(2)}) collective-permute-start(f32[16,256]{1,0:T(8,128)S(1)} %get-tuple-element.52), channel_id=1, source_target_pairs={{0,2},{2,4},{4,6},{6,8},{8,10},{10,12},{12,14},{14,16},{16,18},{18... | collective-permute-start | bytes 49160 | tf_op jit(solution)/shard_map/ppermute | solution.py:455
  6.8 5.0 %collective-permute-start.1 = (f32[16,256]{1,0:T(8,128)S(1)}, f32[16,256]{1,0:T(8,128)S(1)}, u32[]{:S(2)}, u32[]{:S(2)}) collective-permute-start(f32[16,256]{1,0:T(8,128)S(1)} %get-tuple-element.53), channel_id=1, source_target_pairs={{2,0},{4,2},{6,4},{8,6},{10,8},{12,10},{14,12},{16,14},{18,16},{20... | collective-permute-start | bytes 49160 | tf_op jit(solution)/shard_map/ppermute | solution.py:455
  11.9 1.9 %collective-permute-start.2 = (f32[16,256]{1,0:T(8,128)S(1)}, f32[16,256]{1,0:T(8,128)S(1)}, u32[]{:S(2)}, u32[]{:S(2)}) collective-permute-start(f32[16,256]{1,0:T(8,128)S(1)} %get-tuple-element.54), channel_id=1, source_target_pairs={{0,1},{1,0},{2,3},{3,2},{4,5},{5,4},{6,7},{7,6},{8,9},{9,8},{10,11... | collective-permute-start | bytes 49160 | tf_op jit(solution)/shard_map/ppermute | solution.py:454
  13.8 0.0 copy-done.14
  13.8 0.0 copy-done.13
  13.8 0.0 copy-done.10
  13.8 0.0 copy-start.11
  13.9 0.9 %copy-done.11 = f32[4,9,9,32]{3,0,2,1:T(4,128)S(1)} copy-done((f32[4,9,9,32]{3,0,2,1:T(4,128)S(1)}, f32[4,9,9,32]{3,0,2,1:T(4,128)}, u32[]{:S(2)}) %copy-start.11) | copy-done | bytes 41496
  14.7 0.0 copy-start
  14.7 0.0 copy-start.2
  14.8 0.0 copy-start.3
  14.8 0.0 copy-start.5
  14.8 0.0 copy-start.4
  14.8 0.0 copy-start.8
  14.8 0.0 copy-start.9
  14.8 0.8 %copy-done = f32[4,56,56]{2,1,0:T(8,128)S(1)} copy-done((f32[4,56,56]{2,1,0:T(8,128)S(1)}, f32[4,56,56]{2,1,0:T(8,128)}, u32[]{:S(2)}) %copy-start) | copy-done | bytes 50200
  15.6 0.0 copy-done.2
  15.7 0.0 copy-done.3
  15.7 0.0 copy-done.5
  15.7 0.0 copy-done.4
  15.7 0.0 copy-done.8
  15.7 0.0 copy-done.9
  15.7 1.7 %side.1 = (f32[56,384]{1,0:T(8,128)S(1)}, f32[112,384]{1,0:T(8,128)S(1)}, f32[144,128]{1,0:T(8,128)S(1)}, bf16[112,400]{1,0:T(8,128)(2,1)S(1)}, bf16[112,288]{1,...) custom-call(f32[56,384]{1,0:T(8,128)S(1)} %get-tuple-element.37.firs, ...), custom_call_target="tpu_custom_call" | custom-call | flops 2000000000 | bytes 2000000 | tf_op jit(solution)/shard_map/side/pallas_call | solution.py:437
  17.4 0.0 collective-permute-done.fw
  17.5 0.0 collective-permute-done.1.bw
  17.5 0.0 collective-permute-done.2.refs_0_
  17.5 3.8 %middle.1 = (f32[224,128]{1,0:T(8,128)S(1)}, f32[56,384]{1,0:T(8,128)S(1)}, f32[56,384]{1,0:T(8,128)S(1)}, f32[256,128]{1,0:T(8,128)S(1)}, f32[16,256]{1,0:T(8,1...) custom-call(f32[56,384]{1,0:T(8,128)S(1)} %get-tuple-element.39.state, ...), custom_call_target="tpu_custom_call" | custom-call | flops 2000000000 | bytes 2000000 | tf_op jit(solution)/shard_map/middle/pallas_call | solution.py:437
  21.3 0.1 collective-permute-start.3
  21.4 4.4 %collective-permute-start.4 = (f32[16,256]{1,0:T(8,128)S(1)}, f32[16,256]{1,0:T(8,128)S(1)}, u32[]{:S(2)}, u32[]{:S(2)}) collective-permute-start(f32[16,256]{1,0:T(8,128)S(1)} %get-tuple-element.67), channel_id=1, source_target_pairs={{2,0},{4,2},{6,4},{8,6},{10,8},{12,10},{14,12},{16,14},{18,16},{20... | collective-permute-start | bytes 49160 | tf_op jit(solution)/shard_map/ppermute | solution.py:455
  25.8 0.2 collective-permute-start.5
  26.0 0.8 %late_side.1 = (f32[56,384]{1,0:T(8,128)S(1)}, f32[224,128]{1,0:T(8,128)S(1)}) custom-call(f32[56,384]{1,0:T(8,128)S(1)} %get-tuple-element.37.first_in.first, f32[56,384]{1,0:T(8,128)S(1)} %get-tuple-element.38.second, f32[56,384]{1,0:T(8,128)S(1)} %get-tuple-element.55.later, f32[56,384]{1,0:T(8,128)S(1)} %get-tuple-element.56.half, ...), custom_call_target="tpu_custom_call" | custom-call | flops 2000000000 | bytes 2000000 | tf_op jit(solution)/shard_map/late_side/pallas_call | solution.py:437
  26.8 0.4 %collective-permute-done.3.fw = f32[16,256]{1,0:T(8,128)S(1)} collective-permute-done((f32[16,256]{1,0:T(8,128)S(1)}, f32[16,256]{1,0:T(8,128)S(1)}, u32[]{:S(2)}, u32[]{:S(2)}) %collective-permute-start.3) | collective-permute-done | bytes 16416 | tf_op jit(solution)/shard_map/ppermute | solution.py:455
  27.2 0.0 collective-permute-done.4.bw
  27.3 2.3 %collective-permute-done.5.refs_0_ = f32[16,256]{1,0:T(8,128)S(1)} collective-permute-done((f32[16,256]{1,0:T(8,128)S(1)}, f32[16,256]{1,0:T(8,128)S(1)}, u32[]{:S(2)}, u32[]{:S(2)}) %collective-permute-start.5) | collective-permute-done | bytes 16416 | tf_op jit(solution)/shard_map/ppermute | solution.py:454
  29.6 0.8 %last.1 = f32[9,56,32]{2,1,0:T(8,128)S(1)} custom-call(f32[56,384]{1,0:T(8,128)S(1)} %get-tuple-element.63.base, f32[224,128]{1,0:T(8,128)S(1)} %get-tuple-element.64.here, f32[144,128]{1,0:T(8,128)S(1)} %get-tuple-element.44.fnbr, s32[8,128]{1,0:T(8,128)S(1)} %get-tuple-element.45.flags, bf16[112,288]{1,0:T(8,128)(2,1)S(1)} %get-tuple-element.46.lift, ...), custom_call_target="tpu_custom_call" | custom-call | flops 2000000000 | bytes 2000000 | tf_op jit(solution)/shard_map/last/pallas_call | solution.py:437
  30.3 0.8 %copy.25 = f32[9,56,32]{1,2,0:T(8,128)} copy(f32[9,56,32]{2,1,0:T(8,128)S(1)} %last.1) | data formatting | bytes 129024 | tf_op jit(solution)/shard_map/last/pallas_call | solution.py:437
  (4 shorter events, 0.1 us)
Async XLA Ops:
  0.9 1.0 %copy-start.12 = (f32[9,56,32]{1,2,0:T(8,128)S(1)}, f32[9,56,32]{1,2,0:T(8,128)}, u32[]{:S(2)}) copy-start(f32[9,56,32]{1,2,0:T(8,128)} %param.17) | copy-start | bytes 193540
  1.9 0.9 %copy-start.1 = (f32[3,56,56]{2,1,0:T(8,128)S(1)}, f32[3,56,56]{2,1,0:T(8,128)}, u32[]{:S(2)}) copy-start(f32[3,56,56]{2,1,0:T(8,128)} %stiff_in.1) | copy-start | bytes 112900
  1.9 0.9 %copy-start.6 = (s32[1,1,52]{2,1,0:T(1,128)S(1)}, s32[1,1,52]{2,1,0:T(1,128)}, u32[]{:S(2)}) copy-start(s32[1,1,52]{2,1,0:T(1,128)} %elem_in.1) | copy-start | bytes 628
  1.9 0.9 %copy-start.7 = (s32[1,1,52]{2,1,0:T(1,128)S(1)}, s32[1,1,52]{2,1,0:T(1,128)}, u32[]{:S(2)}) copy-start(s32[1,1,52]{2,1,0:T(1,128)} %face_in.1) | copy-start | bytes 628
  2.8 11.0 %copy-start.14 = (f32[4,21,56]{2,0,1:T(4,128)S(1)}, f32[4,21,56]{2,0,1:T(4,128)}, u32[]{:S(2)}) copy-start(f32[4,21,56]{2,0,1:T(4,128)} %param.26) | copy-start | bytes 56452
  2.8 11.0 %copy-start.13 = (f32[16,9,56]{2,0,1:T(8,128)S(1)}, f32[16,9,56]{2,0,1:T(8,128)}, u32[]{:S(2)}) copy-start(f32[16,9,56]{2,0,1:T(8,128)} %param.33) | copy-start | bytes 96772
  6.3 7.5 %copy-start.10 = (f32[4,9,9,32]{3,0,2,1:T(4,128)S(1)}, f32[4,9,9,32]{3,0,2,1:T(4,128)}, u32[]{:S(2)}) copy-start(f32[4,9,9,32]{3,0,2,1:T(4,128)} %param.19) | copy-start | bytes 124420
  6.3 11.2 %collective-permute-start = (f32[16,256]{1,0:T(8,128)S(1)}, f32[16,256]{1,0:T(8,128)S(1)}, u32[]{:S(2)}, u32[]{:S(2)}) collective-permute-start(f32[16,256]{1,0:T(8,128)S(1)} %get-tuple-element.52), channel_id=1, source_target_pairs={{0,2},{2,4},{4,6},{6,8},{8,10},{10,12},{12,14},{14,16},{16,18},{18... | collective-permute-start | bytes 49160 | tf_op jit(solution)/shard_map/ppermute | solution.py:455
  6.8 10.6 %collective-permute-start.1 = (f32[16,256]{1,0:T(8,128)S(1)}, f32[16,256]{1,0:T(8,128)S(1)}, u32[]{:S(2)}, u32[]{:S(2)}) collective-permute-start(f32[16,256]{1,0:T(8,128)S(1)} %get-tuple-element.53), channel_id=1, source_target_pairs={{2,0},{4,2},{6,4},{8,6},{10,8},{12,10},{14,12},{16,14},{18,16},{20... | collective-permute-start | bytes 49160 | tf_op jit(solution)/shard_map/ppermute | solution.py:455
  11.9 5.6 %collective-permute-start.2 = (f32[16,256]{1,0:T(8,128)S(1)}, f32[16,256]{1,0:T(8,128)S(1)}, u32[]{:S(2)}, u32[]{:S(2)}) collective-permute-start(f32[16,256]{1,0:T(8,128)S(1)} %get-tuple-element.54), channel_id=1, source_target_pairs={{0,1},{1,0},{2,3},{3,2},{4,5},{5,4},{6,7},{7,6},{8,9},{9,8},{10,11... | collective-permute-start | bytes 49160 | tf_op jit(solution)/shard_map/ppermute | solution.py:454
  13.8 0.9 %copy-start.11 = (f32[4,9,9,32]{3,0,2,1:T(4,128)S(1)}, f32[4,9,9,32]{3,0,2,1:T(4,128)}, u32[]{:S(2)}) copy-start(f32[4,9,9,32]{3,0,2,1:T(4,128)} %param.20) | copy-start | bytes 124420
  14.7 0.9 %copy-start = (f32[4,56,56]{2,1,0:T(8,128)S(1)}, f32[4,56,56]{2,1,0:T(8,128)}, u32[]{:S(2)}) copy-start(f32[4,56,56]{2,1,0:T(8,128)} %minus_in.1) | copy-start | bytes 150532
  14.7 0.9 %copy-start.2 = (f32[3,56,56]{2,1,0:T(8,128)S(1)}, f32[3,56,56]{2,1,0:T(8,128)}, u32[]{:S(2)}) copy-start(f32[3,56,56]{2,1,0:T(8,128)} %vol_in.1) | copy-start | bytes 112900
  14.8 0.9 %copy-start.3 = (f32[3,21,21]{2,1,0:T(8,128)S(1)}, f32[3,21,21]{2,1,0:T(8,128)}, u32[]{:S(2)}) copy-start(f32[3,21,21]{2,1,0:T(8,128)} %turn_in.1) | copy-start | bytes 15880
  14.8 0.9 %copy-start.5 = (s32[4,32]{1,0:T(4,128)S(1)}, s32[4,32]{1,0:T(4,128)}, u32[]{:S(2)}) copy-start(s32[4,32]{1,0:T(4,128)} %orient_in.1) | copy-start | bytes 1540
  14.8 0.9 %copy-start.4 = (s32[4,32]{1,0:T(4,128)S(1)}, s32[4,32]{1,0:T(4,128)}, u32[]{:S(2)}) copy-start(s32[4,32]{1,0:T(4,128)} %index_in.1) | copy-start | bytes 1540
  14.8 0.9 %copy-start.8 = (s32[32]{0:T(128)S(1)}, s32[32]{0:T(128)}, u32[]{:S(2)}) copy-start(s32[32]{0:T(128)} %param.27) | copy-start | bytes 388
  14.8 0.9 %copy-start.9 = (s32[16]{0:T(128)S(1)}, s32[16]{0:T(128)}, u32[]{:S(2)}) copy-start(s32[16]{0:T(128)} %source_elem.1) | copy-start | bytes 196
  21.3 5.9 %collective-permute-start.3 = (f32[16,256]{1,0:T(8,128)S(1)}, f32[16,256]{1,0:T(8,128)S(1)}, u32[]{:S(2)}, u32[]{:S(2)}) collective-permute-start(f32[16,256]{1,0:T(8,128)S(1)} %get-tuple-element.66), channel_id=1, source_target_pairs={{0,2},{2,4},{4,6},{6,8},{8,10},{10,12},{12,14},{14,16},{16,18},{18... | collective-permute-start | bytes 49160 | tf_op jit(solution)/shard_map/ppermute | solution.py:455
  21.4 5.9 %collective-permute-start.4 = (f32[16,256]{1,0:T(8,128)S(1)}, f32[16,256]{1,0:T(8,128)S(1)}, u32[]{:S(2)}, u32[]{:S(2)}) collective-permute-start(f32[16,256]{1,0:T(8,128)S(1)} %get-tuple-element.67), channel_id=1, source_target_pairs={{2,0},{4,2},{6,4},{8,6},{10,8},{12,10},{14,12},{16,14},{18,16},{20... | collective-permute-start | bytes 49160 | tf_op jit(solution)/shard_map/ppermute | solution.py:455
  25.8 3.7 %collective-permute-start.5 = (f32[16,256]{1,0:T(8,128)S(1)}, f32[16,256]{1,0:T(8,128)S(1)}, u32[]{:S(2)}, u32[]{:S(2)}) collective-permute-start(f32[16,256]{1,0:T(8,128)S(1)} %get-tuple-element.68), channel_id=1, source_target_pairs={{0,1},{1,0},{2,3},{3,2},{4,5},{5,4},{6,7},{7,6},{8,9},{9,8},{10,11... | collective-permute-start | bytes 49160 | tf_op jit(solution)/shard_map/ppermute | solution.py:454
where the time goes:
time: 31.4 us; the launch traced here: 31.1 us
  starting transfers between devices  12.1 us (39%)
  Pallas kernels  10.6 us (34%)
  local copies, waits for them, and re-layouts  5.41 us (17%)
  waiting for transfers between devices  2.76 us (9%)
    pallas_call x5, Pallas kernels, call(): pl.pallas_call(kernel, in_specs=specs, out_specs=[pl.BlockSpec(memory_spa...  10.6 us
    ppermute x4, starting transfers between devices, trade(): return (lax.ppermute(fw, 'fault', up), lax.ppermute(bw, 'fault', down), got)  10.1 us
    unnamed x37, local copies, waits for them, and re-layouts  4.61 us
    ppermute x2, waiting for transfers between devices, trade(): lax.ppermute(rows, 'off', [(j, (j + k) % n_off) for j in range(n_off)])  2.3 us
    ppermute x2, starting transfers between devices, trade(): lax.ppermute(rows, 'off', [(j, (j + k) % n_off) for j in range(n_off)])  2.03 us
    pallas_call x1, local copies, waits for them, and re-layouts, call(): pl.pallas_call(kernel, in_specs=specs, out_specs=[pl.BlockSpec(memory_spa...  0.8 us
  transfers between devices with their start and end apart: 6, of which 2 were waited for; matrix products, arithmetic and copies ran while one was open for 0% of the time, Pallas kernels for 8%

commit v1 on v0

--- a/solution.py
+++ b/solution.py
@@ -7,6 +7,7 @@
 from jax.experimental import pallas as pl
 from jax.experimental.pallas import tpu as pltpu
 from jax.sharding import PartitionSpec as P
+
 
 Q = 9
 M = 56
@@ -15,7 +16,6 @@
 E = 32
 LANES = 128
 W = 384
-SF = 16
 SO = 10
 SRC = 16
 TERMS = 6
@@ -97,16 +97,9 @@
 
 
 def group_place(parts):
-    total = parts[0]
-    for group, part in enumerate(parts[1:], 1):
-        total = total + roll(part, 32 * group)
-    return total
-
-
-def widen(x, pad):
-    rows = x.shape[0]
-    pad[0:rows, 0:E] = x
-    return pad[0:rows, :]
+    if len(parts) < 4:
+        parts = parts + [jnp.zeros((parts[0].shape[0], E * (4 - len(parts))), parts[0].dtype)]
+    return jnp.concatenate(parts, axis=1)
 
 
 def weigh(rows_of, x_ref, y_ref, count):
@@ -176,37 +169,43 @@
         ref[...] = rows[48 + 16 * k : 64 + 16 * k]
 
 
-def first_kernel(n_off, state_in, star_in, stiff_in, proj_in, elem_in, face_in, *refs):
+def first_kernel(n_off, *refs):
+    sources = refs[:6]
+    landed = refs[-7:-1]
+    copies = [
+        pltpu.make_async_copy(source, target, refs[-1].at[k])
+        for k, (source, target) in enumerate(zip(sources, landed))
+    ]
+    for copy in copies:
+        copy.start()
+    state_in, star_in, stiff_in, proj_in, elem_in, face_in = landed
+    refs = refs[6:-7]
     (state_out, first_out, second_out, star_out, left_out, proj_out, tab_out, pick_out, bw, fw, own) = refs[:11]
     offs = refs[11 : 11 + n_off - 1]
-    x_ref, y_ref, pad, high_pad, slot_pad = refs[11 + n_off - 1 :]
-    pad[...] = jnp.zeros((64, LANES), F32)
-    for c in range(3):
-        parts = [widen(state_in[q], pad) for q in range(4 * c, min(4 * c + 4, Q))]
-        column = group_place(parts)
-        x_ref[:, c * 128 : c * 128 + 128] = column
-        state_out[:, c * 128 : c * 128 + 128] = column
-    pad[...] = jnp.zeros((64, LANES), F32)
+    x_ref, y_ref, tall, slot_pad = refs[11 + n_off - 1 :]
+    tall[...] = jnp.zeros((W, LANES), F32)
+    slot_pad[...] = jnp.zeros((8, LANES), jnp.int32)
+    for copy in copies:
+        copy.wait()
+    for q in range(Q):
+        tall[q * E : q * E + E, 0:M] = state_in[q]
+    state = tall[...].T[0:M, :]
+    x_ref[...] = state
+    state_out[...] = state
     for d in range(3):
         for c in range(3):
-            parts = []
-            for q in range(4 * c, min(4 * c + 4, Q)):
-                pad[0:Q, 0:E] = star_in[d, q]
-                parts.append(pad[0:16, :])
-            star_out[d * 16 : d * 16 + 16, c * 128 : c * 128 + 128] = group_place(parts)
-    high_pad[...] = jnp.zeros((256, LANES), F32)
+            star_out[d * 16 : d * 16 + Q, c * 128 : c * 128 + 128] = group_place(
+                [star_in[q, :, d, :] for q in range(4 * c, min(4 * c + 4, Q))]
+            )
+    tall[...] = jnp.zeros((W, LANES), F32)
     for d in range(3):
-        high_pad[d * M : d * M + M, 0:M] = stiff_in[d]
-    left_out[...] = stack_split(high_pad[...].T[0:M, 0 : 3 * M + 8])
-    high_pad[...] = jnp.zeros((256, LANES), F32)
+        tall[d * M : d * M + M, 0:M] = stiff_in[d]
+    left_out[...] = stack_split(tall[0:256, :].T[0:M, 0 : 3 * M + 8])
+    tall[0 : 4 * JP, :] = jnp.zeros((4 * JP, LANES), F32)
     for f in range(4):
-        high_pad[f * 64 : f * 64 + M, 0:J] = proj_in[f]
-    turned = high_pad[...].T
-    proj_out[...] = stack_split(
-        jnp.concatenate([turned[0:JP, f * 64 : f * 64 + M] for f in range(4)], axis=0)
-    )
+        tall[f * JP : f * JP + J, 0:M] = proj_in[:, f, :]
+    proj_out[...] = stack_split(tall[0 : 4 * JP, 0:M])
     slots = elem_in.shape[2]
-    slot_pad[...] = jnp.zeros((8, LANES), jnp.int32)
     slot_pad[0:1, 0:slots] = face_in[0] * E + elem_in[0] + 1
     rows = 32 + 16 * n_off
     row = row_iota(rows)
@@ -256,28 +255,19 @@
     flags_out,
     source_out,
     y_ref,
-    pad,
     tall,
     turn_pad,
     lift_pad,
     ipad,
 ):
-    pad[...] = jnp.zeros((64, LANES), F32)
-    for d in range(3):
-        coef_out[d * 16 : d * 16 + 16, :] = star[d * 16 : d * 16 + 16, :]
+    coef_out[0:48, :] = star[...]
     for f in range(4):
         for c in range(3):
-            parts = []
-            for q in range(4 * c, min(4 * c + 4, Q)):
-                pad[0:Q, 0:E] = local_in[f, q]
-                parts.append(pad[0:16, :])
-            coef_out[(3 + f) * 16 : (4 + f) * 16, c * 128 : c * 128 + 128] = group_place(parts)
+            coef_out[(3 + f) * 16 : (3 + f) * 16 + Q, c * 128 : c * 128 + 128] = group_place(
+                [local_in[q, :, f, :] for q in range(4 * c, min(4 * c + 4, Q))]
+            )
     for q in range(Q):
-        parts = []
-        for f in range(4):
-            pad[0:Q, 0:E] = nbr_in[f, q]
-            parts.append(pad[0:16, :])
-        fnbr_out[q * 16 : q * 16 + 16, :] = group_place(parts)
+        fnbr_out[q * 16 : q * 16 + Q, :] = group_place([nbr_in[q, :, f, :] for f in range(4)])
     tall[...] = jnp.zeros((512, LANES), F32)
     for d in range(3):
         tall[d * M : d * M + M, 0:M] = vol_in[d]
@@ -290,7 +280,7 @@
     tall[...] = jnp.zeros((512, LANES), F32)
     lift_pad[...] = jnp.zeros((LANES, LANES), F32)
     for f in range(4):
-        lift_pad[0:J, 0:M] = lift_in[f]
+        lift_pad[0:J, 0:M] = lift_in[:, f, :]
         tall[f * 3 * JP : (f + 1) * 3 * JP, :] = lax.dot_general(
             turn_pad[...],
             lift_pad[...],
@@ -300,8 +290,7 @@
         )
     lift_out[...] = stack_split(tall[...].T[0:M, 0 : 12 * JP])
     ipad[...] = jnp.zeros((8, LANES), jnp.int32)
-    ipad[0:4, 0:E] = index_in[...]
-    index_row = group_place([ipad[f : f + 1, :] for f in range(4)])
+    index_row = group_place([index_in[f : f + 1, :] for f in range(4)])
     ipad[0:4, 0:E] = orient_in[...]
     ipad[4:5, 0:E] = cluster_in[...]
     orient = ipad[...]
@@ -319,29 +308,32 @@
     pick_far_out[...] = jnp.where(place == index_row, 1.0, 0.0).astype(BF16)
     here_out[...] = gather_local(pick_here, tab)
     tall[...] = jnp.zeros((512, LANES), F32)
+    for q in range(Q):
+        tall[q * SRC : q * SRC + SRC, 0:M] = source_in[q]
+    origin = (lax.axis_index("fault") * n_off + off_rank()) * E
+    row = row_iota(SRC)
+    goal = jnp.full((SRC, LANES), -1, jnp.int32)
     for s in range(SRC):
-        tall[s * 16 : s * 16 + Q, 0:M] = source_in[s]
-    origin = (lax.axis_index("fault") * n_off + off_rank()) * E
-    row16 = row_iota(16, W)
-    lane16 = lane_iota(16, W)
-    for s in range(SRC):
-        spot = source_elem[s] - origin
-        inside = jnp.logical_and(spot >= 0, spot < E)
-        goal = jnp.where(inside, spot, -100000)
-        y_ref[s * 16 : s * 16 + 16, :] = jnp.where(
-            jnp.logical_and(lane16 == row16 * E + goal, row16 < Q), 1.0, 0.0
-        )
-    picks = y_ref[0 : SRC * 16, :].astype(BF16)
-    high, low = split(tall[...].T[0:M, 0 : SRC * 16])
-    rest = tall[...].T[0:M, 0 : SRC * 16] - high.astype(F32) - low.astype(F32)
-    source_out[...] = dot(high, picks) + (dot(low, picks) + dot(rest.astype(BF16), picks))
+        goal = jnp.where(row == s, source_elem[s] - origin, goal)
+    y_ref[0 : Q * SRC, :] = jnp.zeros((Q * SRC, W), F32)
+    lane = lane_iota(SRC)
+    for q in range(Q):
+        lane_in = lane - 32 * (q % 4)
+        hit = jnp.logical_and(lane_in == goal, jnp.logical_and(goal >= 0, goal < E))
+        c = q // 4
+        y_ref[q * SRC : q * SRC + SRC, c * 128 : c * 128 + 128] = jnp.where(hit, 1.0, 0.0)
+    picks = y_ref[0 : Q * SRC, :].astype(BF16)
+    terms = tall[0:256, :].T[0:M, 0 : Q * SRC]
+    high, low = split(terms)
+    rest = (terms - high.astype(F32) - low.astype(F32)).astype(BF16)
+    source_out[...] = dot(high, picks) + (dot(low, picks) + dot(rest, picks))
 
     weigh(coef_out, first_in, y_ref, 7)
     y_ref[7 * M : 7 * M + 8, :] = jnp.zeros((8, W), F32)
     part_out[...] = product(left_out[...], y_ref[...])
 
 
-def arrive(n_off, fw, bw, own, offs, pick_far, stage):
+def arrive(fw, bw, own, offs, pick_far, stage):
     stage[0:16, :] = fw[...]
     stage[16:32, :] = bw[...]
     stage[32:48, :] = own[...]
@@ -388,7 +380,7 @@
     near_out, half_out, later_out, tab_out, bw_out, fw_out, own_out = outs[:7]
     off_outs = outs[7 : 7 + n_off - 1]
     x_ref, y_ref, stage, acc = outs[7 + n_off - 1 :]
-    near_out[...] = here[...] + arrive(n_off, fw, bw, own, offs, pick_far, stage)
+    near_out[...] = here[...] + arrive(fw, bw, own, offs, pick_far, stage)
     total = part[...] + neighbour_flux(near_out, fnbr, flags, lift, y_ref)
     fine = jnp.concatenate([wide_fine(flags)] * 3, axis=1)
     base = state[...]
@@ -416,23 +408,26 @@
 
 def last_kernel(n_off, base, here, fnbr, flags, lift, pick_far, own, fw, bw, *refs):
     offs = refs[: n_off - 1]
-    out, near, y_ref, stage = refs[n_off - 1 :]
-    near[...] = here[...] + arrive(n_off, fw, bw, own, offs, pick_far, stage)
+    out, near, y_ref, stage, tall = refs[n_off - 1 :]
+    tall[M:LANES, :] = jnp.zeros((LANES - M, W), F32)
+    near[...] = here[...] + arrive(fw, bw, own, offs, pick_far, stage)
     total = base[...] + neighbour_flux(near, fnbr, flags, lift, y_ref)
+    tall[0:M, :] = total
+    turned = tall[...].T
     for q in range(Q):
-        column = total[:, (q // 4) * 128 : (q // 4) * 128 + 128]
-        if q % 4:
-            column = roll(column, 128 - 32 * (q % 4))
-        out[q] = column[:, 0:E]
+        out[q] = turned[q * E : q * E + E, 0:M]
 
 
 def shape(*dims, dtype=F32):
     return jax.ShapeDtypeStruct(dims, dtype)
 
 
-def call(kernel, ins, outs, scratch, name, smem=(), cost=2000000):
+def call(kernel, ins, outs, scratch, smem=(), hbm=(), cost=2000000):
     specs = [
-        pl.BlockSpec(memory_space=pltpu.SMEM if k in smem else pltpu.VMEM) for k in range(len(ins))
+        pl.BlockSpec(
+            memory_space=pltpu.SMEM if k in smem else pltpu.HBM if k in hbm else pltpu.VMEM
+        )
+        for k in range(len(ins))
     ]
     return pl.pallas_call(
         kernel,
@@ -440,7 +435,6 @@
         out_specs=[pl.BlockSpec(memory_space=pltpu.VMEM)] * len(outs),
         out_shape=outs,
         scratch_shapes=scratch,
-        name=name,
         compiler_params=pltpu.CompilerParams(vmem_limit_bytes=16 * 1024 * 1024),
         cost_estimate=pl.CostEstimate(flops=cost * 1000, bytes_accessed=cost, transcendentals=0),
     )(*ins)
@@ -452,7 +446,9 @@
     got = []
     for k, rows in enumerate(offs, 1):
         got.append(lax.ppermute(rows, "off", [(j, (j + k) % n_off) for j in range(n_off)]))
-    return lax.ppermute(fw, "fault", up), lax.ppermute(bw, "fault", down), got
+    ahead = lax.ppermute(fw, "fault", up)
+    behind = lax.ppermute(bw, "fault", down)
+    return ahead, behind, got
 
 
 def on_device(
@@ -482,9 +478,17 @@
     table = shape(TAB, LANES)
     block = shape(16, TAB)
     near = shape(Q * JP + 8, LANES)
+    given = (
+        jnp.transpose(modal_state, (0, 2, 1)),
+        jnp.transpose(star_mats, (1, 2, 0, 3)),
+        stiff_time,
+        jnp.transpose(face_proj, (2, 0, 1)),
+        send_elem,
+        send_face,
+    )
     outs = call(
         functools.partial(first_kernel, n_off),
-        (modal_state, star_mats, stiff_time, face_proj, send_elem, send_face),
+        [pltpu.with_memory_space_constraint(x, pltpu.HBM) for x in given],
         [
             wide,
             wide,
@@ -499,11 +503,12 @@
         [
             vmem((M, W), F32),
             vmem((3 * M + 8, W), F32),
-            vmem((64, LANES), F32),
-            vmem((256, LANES), F32),
+            vmem((W, LANES), F32),
             vmem((8, LANES), jnp.int32),
-        ],
-        "first",
+        ]
+        + [vmem(x.shape, x.dtype) for x in given]
+        + [pltpu.SemaphoreType.DMA((len(given),))],
+        hbm=range(len(given)),
     )
     state, first, second, star, left, proj, tab, pick, bw, fw, own = outs[:11]
     got_fw, got_bw, got_off = trade(bw, fw, outs[11:], n_fault, n_off)
@@ -513,17 +518,17 @@
             first,
             star,
             tab,
-            flux_local,
-            flux_nbr,
+            jnp.transpose(flux_local, (1, 2, 0, 3)),
+            jnp.transpose(flux_nbr, (1, 2, 0, 3)),
             stiff_vol,
             flux_minus,
             face_turn,
-            face_lift,
+            jnp.transpose(face_lift, (1, 0, 2)),
             nbr_index,
             orientation,
             cluster.reshape(1, E),
             source_elem,
-            source_term,
+            jnp.transpose(source_term, (1, 0, 2)),
         ),
         [
             wide,
@@ -539,13 +544,11 @@
         ],
         [
             vmem((7 * M + 8, W), F32),
-            vmem((64, LANES), F32),
             vmem((512, LANES), F32),
             vmem((3 * JP, LANES), F32),
             vmem((LANES, LANES), F32),
             vmem((8, LANES), jnp.int32),
         ],
-        "side",
         smem=(12,),
     )
     outs = call(
@@ -553,7 +556,6 @@
         (state, second, part, here, fnbr, flags, lift, star, left, proj, pick, pick_far, own, got_fw, got_bw, *got_off),
         [near, wide, wide, table] + [block] * (3 + n_off - 1),
         [vmem((M, W), F32), vmem((12 * JP, W), F32), vmem((rows, TAB), F32), vmem((M, W), F32)],
-        "middle",
     )
     near_first, half, later, tab, bw, fw, own = outs[:7]
     got_fw, got_bw, got_off = trade(bw, fw, outs[7:], n_fault, n_off)
@@ -562,16 +564,14 @@
         (first, second, later, half, source, near_first, tab, coef, left_all, flags, pick_here),
         [wide, near],
         [vmem((M, W), F32), vmem((7 * M + 8, W), F32)],
-        "late_side",
     )
     (result,) = call(
         functools.partial(last_kernel, n_off),
         (base, here, fnbr, flags, lift, pick_far, own, got_fw, got_bw, *got_off),
-        [shape(Q, M, E)],
-        [vmem((Q * JP + 8, LANES), F32), vmem((12 * JP, W), F32), vmem((rows, TAB), F32)],
-        "last",
-    )
-    return result
+        [shape(Q, E, M)],
+        [vmem((Q * JP + 8, LANES), F32), vmem((12 * JP, W), F32), vmem((rows, TAB), F32), vmem((LANES, W), F32)],
+    )
+    return jnp.transpose(result, (0, 2, 1))
 
 
 def solution(mesh):

time: 31.4 us -> 28.1 us (0.89)
  local copies, waits for them, and re-layouts: 5.41 us -> 0.64 us
  Pallas kernels: 10.6 us -> 12.3 us
  starting transfers between devices: 12.1 us -> 13.3 us
  waiting for transfers between devices: 2.76 us -> 1.56 us
    unnamed x37 -> x22, local copies, waits for them, and re-layouts: 4.61 us -> 0.64 us
    pallas_call x5, Pallas kernels: 10.6 us -> 12.3 us  [call(): pl.pallas_call(kernel, in_specs=specs, out_specs=[pl.BlockSpec(memory_spa...]
    ppermute x2, starting transfers between devices: 2.03 us -> 3.23 us  [trade(): lax.ppermute(rows, 'off', [(j, (j + k) % n_off) for j in range(n_off)])]
    pallas_call x1 -> x0, local copies, waits for them, and re-layouts: 0.8 us -> none  [call(): pl.pallas_call(kernel, in_specs=specs, out_specs=[pl.BlockSpec(memory_spa...]
    ppermute x2, waiting for transfers between devices: 2.3 us -> 1.55 us  [trade(): lax.ppermute(rows, 'off', [(j, (j + k) % n_off) for j in range(n_off)])]
    ppermute x4, waiting for transfers between devices: 0.47 us -> 0.01 us  [the longest x2 0.01 us: trade(): behind = lax.ppermute(bw, 'fault', down)]
  transfers between devices with their start and end apart: 6 -> 6, of which waited for: 2 -> 1; matrix products, arithmetic and copies ran while one was open for 0% -> 0% of each run, Pallas kernels for 8% -> 9%
where the time goes in v1:
time: 28.1 us; the launch traced here: 28 us
  starting transfers between devices  13.3 us (47%)
  Pallas kernels  12.3 us (44%)
  waiting for transfers between devices  1.56 us (6%)
  local copies, waits for them, and re-layouts  0.64 us (2%)
    pallas_call x5, Pallas kernels, call(): pl.pallas_call(kernel, in_specs=specs, out_specs=[pl.BlockSpec(memory_spa...  12.3 us
    ppermute x2, starting transfers between devices, trade(): behind = lax.ppermute(bw, 'fault', down)  9.48 us
    ppermute x2, starting transfers between devices, trade(): lax.ppermute(rows, 'off', [(j, (j + k) % n_off) for j in range(n_off)])  3.23 us
    ppermute x2, waiting for transfers between devices, trade(): lax.ppermute(rows, 'off', [(j, (j + k) % n_off) for j in range(n_off)])  1.55 us
    unnamed x22, local copies, waits for them, and re-layouts  0.64 us
    ppermute x2, starting transfers between devices, trade(): ahead = lax.ppermute(fw, 'fault', up)  0.64 us
  transfers between devices with their start and end apart: 6, of which 1 were waited for; matrix products, arithmetic and copies ran while one was open for 0% of the time, Pallas kernels for 9%

profile of v1, /device:TPU:0, one launch (start us, length us, event | category | flops | bytes accessed | tf_op | source)
XLA Modules:
  0.0 28.0 jit_solution(9844439087204722720)
XLA Ops:
  0.0 0.0 copy-start
  0.0 0.0 copy-start.1
  0.0 0.0 copy-start.2
  0.0 0.0 copy-start.3
  0.0 0.0 copy-start.4
  0.0 0.0 copy-start.5
  0.0 0.0 copy-start.6
  0.0 0.0 copy-start.8
  0.0 4.5 %shard_map.163 = (f32[56,384]{1,0:T(8,128)S(1)}, f32[56,384]{1,0:T(8,128)S(1)}, f32[56,384]{1,0:T(8,128)S(1)}, f32[48,384]{1,0:T(8,128)S(1)}, bf16[112,176]{1,0:...) custom-call(f32[9,32,56]{2,1,0:T(8,128)} %bitcast.15, ...), custom_call_target="tpu_custom_call" | custom-call | flops 2000000000 | bytes 2000000 | tf_op jit(solution)/shard_map/pallas_call | solution.py:432
  4.6 0.6 %collective-permute-start = (f32[16,256]{1,0:T(8,128)S(1)}, f32[16,256]{1,0:T(8,128)S(1)}, u32[]{:S(2)}, u32[]{:S(2)}) collective-permute-start(f32[16,256]{1,0:T(8,128)S(1)} %get-tuple-element.52), channel_id=1, source_target_pairs={{0,2},{2,4},{4,6},{6,8},{8,10},{10,12},{12,14},{14,16},{16,18},{18... | collective-permute-start | bytes 49160 | tf_op jit(solution)/shard_map/ppermute | solution.py:449
  5.2 5.0 %collective-permute-start.1 = (f32[16,256]{1,0:T(8,128)S(1)}, f32[16,256]{1,0:T(8,128)S(1)}, u32[]{:S(2)}, u32[]{:S(2)}) collective-permute-start(f32[16,256]{1,0:T(8,128)S(1)} %get-tuple-element.53), channel_id=1, source_target_pairs={{2,0},{4,2},{6,4},{8,6},{10,8},{12,10},{14,12},{16,14},{18,16},{20... | collective-permute-start | bytes 49160 | tf_op jit(solution)/shard_map/ppermute | solution.py:450
  10.2 1.9 %collective-permute-start.2 = (f32[16,256]{1,0:T(8,128)S(1)}, f32[16,256]{1,0:T(8,128)S(1)}, u32[]{:S(2)}, u32[]{:S(2)}) collective-permute-start(f32[16,256]{1,0:T(8,128)S(1)} %get-tuple-element.54), channel_id=1, source_target_pairs={{0,1},{1,0},{2,3},{3,2},{4,5},{5,4},{6,7},{7,6},{8,9},{9,8},{10,11... | collective-permute-start | bytes 49160 | tf_op jit(solution)/shard_map/ppermute | solution.py:448
  12.1 0.0 copy-start.7
  12.1 0.0 copy-start.9
  12.1 0.0 copy-start.10
  12.1 0.0 copy-done
  12.1 0.0 copy-done.1
  12.1 0.0 copy-done.2
  12.1 0.0 copy-done.3
  12.1 0.0 copy-done.4
  12.1 0.0 copy-done.5
  12.1 0.0 copy-done.6
  12.2 0.0 copy-done.8
  12.2 0.6 %copy-done.7 = s32[4,32]{1,0:T(4,128)S(1)} copy-done((s32[4,32]{1,0:T(4,128)S(1)}, s32[4,32]{1,0:T(4,128)}, u32[]{:S(2)}) %copy-start.7) | copy-done | bytes 536
  12.8 0.0 copy-done.9
  12.8 0.0 copy-done.10
  12.8 1.6 %shard_map.164 = (f32[56,384]{1,0:T(8,128)S(1)}, f32[112,384]{1,0:T(8,128)S(1)}, f32[144,128]{1,0:T(8,128)S(1)}, bf16[112,400]{1,0:T(8,128)(2,1)S(1)}, bf16[112,...) custom-call(f32[56,384]{1,0:T(8,128)S(1)} %get-tuple-element.37.firs, ...), custom_call_target="tpu_custom_call" | custom-call | flops 2000000000 | bytes 2000000 | tf_op jit(solution)/shard_map/pallas_call | solution.py:432
  14.4 0.0 collective-permute-done.fw
  14.4 0.0 collective-permute-done.1.bw
  14.4 0.0 collective-permute-done.2.refs_0_
  14.4 3.8 %shard_map.165 = (f32[224,128]{1,0:T(8,128)S(1)}, f32[56,384]{1,0:T(8,128)S(1)}, f32[56,384]{1,0:T(8,128)S(1)}, f32[256,128]{1,0:T(8,128)S(1)}, f32[16,256]{1,0:...) custom-call(f32[56,384]{1,0:T(8,128)S(1)} %get-tuple-element.39.state, ...), custom_call_target="tpu_custom_call" | custom-call | flops 2000000000 | bytes 2000000 | tf_op jit(solution)/shard_map/pallas_call | solution.py:432
  18.3 0.1 collective-permute-start.3
  18.4 4.4 %collective-permute-start.4 = (f32[16,256]{1,0:T(8,128)S(1)}, f32[16,256]{1,0:T(8,128)S(1)}, u32[]{:S(2)}, u32[]{:S(2)}) collective-permute-start(f32[16,256]{1,0:T(8,128)S(1)} %get-tuple-element.67), channel_id=1, source_target_pairs={{2,0},{4,2},{6,4},{8,6},{10,8},{12,10},{14,12},{16,14},{18,16},{20... | collective-permute-start | bytes 49160 | tf_op jit(solution)/shard_map/ppermute | solution.py:450
  22.8 1.4 %collective-permute-start.5 = (f32[16,256]{1,0:T(8,128)S(1)}, f32[16,256]{1,0:T(8,128)S(1)}, u32[]{:S(2)}, u32[]{:S(2)}) collective-permute-start(f32[16,256]{1,0:T(8,128)S(1)} %get-tuple-element.68), channel_id=1, source_target_pairs={{0,1},{1,0},{2,3},{3,2},{4,5},{5,4},{6,7},{7,6},{8,9},{9,8},{10,11... | collective-permute-start | bytes 49160 | tf_op jit(solution)/shard_map/ppermute | solution.py:448
  24.1 0.8 %shard_map.166 = (f32[56,384]{1,0:T(8,128)S(1)}, f32[224,128]{1,0:T(8,128)S(1)}) custom-call(f32[56,384]{1,0:T(8,128)S(1)} %get-tuple-element.37.first_in.first, f32[56,384]{1,0:T(8,128)S(1)} %get-tuple-element.38.second, f32[56,384]{1,0:T(8,128)S(1)} %get-tuple-element.55.later, f32[56,384]{1,0:T(8,128)S(1)} %get-tuple-element.56.half, ...), custom_call_target="tpu_custom_call" | custom-call | flops 2000000000 | bytes 2000000 | tf_op jit(solution)/shard_map/pallas_call | solution.py:432
  25.0 0.0 collective-permute-done.3.fw
  25.0 0.0 collective-permute-done.4.bw
  25.0 1.6 %collective-permute-done.5.refs_0_ = f32[16,256]{1,0:T(8,128)S(1)} collective-permute-done((f32[16,256]{1,0:T(8,128)S(1)}, f32[16,256]{1,0:T(8,128)S(1)}, u32[]{:S(2)}, u32[]{:S(2)}) %collective-permute-start.5) | collective-permute-done | bytes 16416 | tf_op jit(solution)/shard_map/ppermute | solution.py:448
  26.5 1.5 %shard_map.167 = f32[9,32,56]{2,1,0:T(8,128)} custom-call(f32[56,384]{1,0:T(8,128)S(1)} %get-tuple-element.63.base, f32[224,128]{1,0:T(8,128)S(1)} %get-tuple-element.64.here, f32[144,128]{1,0:T(8,128)S(1)} %get-tuple-element.44.fnbr, s32[8,128]{1,0:T(8,128)S(1)} %get-tuple-element.45.flags, bf16[112,288]{1,0:T(8,128)(2,1)S(1)} %get-tuple-element.46.lift, ...), custom_call_target="tpu_custom_call" | custom-call | flops 2000000000 | bytes 2000000 | tf_op jit(solution)/shard_map/pallas_call | solution.py:432
Async XLA Ops:
  0.0 12.1 %copy-start = (f32[4,9,9,32]{3,0,2,1:T(4,128)S(1)}, f32[4,9,9,32]{3,0,2,1:T(4,128)}, u32[]{:S(2)}) copy-start(f32[4,9,9,32]{3,0,2,1:T(4,128)} %param.19) | copy-start | bytes 124420
  0.0 12.1 %copy-start.1 = (f32[4,9,9,32]{3,0,2,1:T(4,128)S(1)}, f32[4,9,9,32]{3,0,2,1:T(4,128)}, u32[]{:S(2)}) copy-start(f32[4,9,9,32]{3,0,2,1:T(4,128)} %param.20) | copy-start | bytes 124420
  0.0 12.1 %copy-start.2 = (f32[4,56,56]{2,1,0:T(8,128)S(1)}, f32[4,56,56]{2,1,0:T(8,128)}, u32[]{:S(2)}) copy-start(f32[4,56,56]{2,1,0:T(8,128)} %minus_in.1) | copy-start | bytes 150532
  0.0 12.1 %copy-start.3 = (f32[3,56,56]{2,1,0:T(8,128)S(1)}, f32[3,56,56]{2,1,0:T(8,128)}, u32[]{:S(2)}) copy-start(f32[3,56,56]{2,1,0:T(8,128)} %vol_in.1) | copy-start | bytes 112900
  0.0 12.1 %copy-start.4 = (f32[16,9,56]{2,0,1:T(8,128)S(1)}, f32[16,9,56]{2,0,1:T(8,128)}, u32[]{:S(2)}) copy-start(f32[16,9,56]{2,0,1:T(8,128)} %param.33) | copy-start | bytes 96772
  0.0 12.1 %copy-start.5 = (f32[4,21,56]{2,0,1:T(4,128)S(1)}, f32[4,21,56]{2,0,1:T(4,128)}, u32[]{:S(2)}) copy-start(f32[4,21,56]{2,0,1:T(4,128)} %param.26) | copy-start | bytes 56452
  0.0 12.1 %copy-start.6 = (f32[3,21,21]{2,1,0:T(8,128)S(1)}, f32[3,21,21]{2,1,0:T(8,128)}, u32[]{:S(2)}) copy-start(f32[3,21,21]{2,1,0:T(8,128)} %turn_in.1) | copy-start | bytes 15880
  0.0 12.1 %copy-start.8 = (s32[4,32]{1,0:T(4,128)S(1)}, s32[4,32]{1,0:T(4,128)}, u32[]{:S(2)}) copy-start(s32[4,32]{1,0:T(4,128)} %orient_in.1) | copy-start | bytes 1540
  4.6 9.8 %collective-permute-start = (f32[16,256]{1,0:T(8,128)S(1)}, f32[16,256]{1,0:T(8,128)S(1)}, u32[]{:S(2)}, u32[]{:S(2)}) collective-permute-start(f32[16,256]{1,0:T(8,128)S(1)} %get-tuple-element.52), channel_id=1, source_target_pairs={{0,2},{2,4},{4,6},{6,8},{8,10},{10,12},{12,14},{14,16},{16,18},{18... | collective-permute-start | bytes 49160 | tf_op jit(solution)/shard_map/ppermute | solution.py:449
  5.2 9.3 %collective-permute-start.1 = (f32[16,256]{1,0:T(8,128)S(1)}, f32[16,256]{1,0:T(8,128)S(1)}, u32[]{:S(2)}, u32[]{:S(2)}) collective-permute-start(f32[16,256]{1,0:T(8,128)S(1)} %get-tuple-element.53), channel_id=1, source_target_pairs={{2,0},{4,2},{6,4},{8,6},{10,8},{12,10},{14,12},{16,14},{18,16},{20... | collective-permute-start | bytes 49160 | tf_op jit(solution)/shard_map/ppermute | solution.py:450
  10.2 4.2 %collective-permute-start.2 = (f32[16,256]{1,0:T(8,128)S(1)}, f32[16,256]{1,0:T(8,128)S(1)}, u32[]{:S(2)}, u32[]{:S(2)}) collective-permute-start(f32[16,256]{1,0:T(8,128)S(1)} %get-tuple-element.54), channel_id=1, source_target_pairs={{0,1},{1,0},{2,3},{3,2},{4,5},{5,4},{6,7},{7,6},{8,9},{9,8},{10,11... | collective-permute-start | bytes 49160 | tf_op jit(solution)/shard_map/ppermute | solution.py:448
  12.1 0.7 %copy-start.7 = (s32[4,32]{1,0:T(4,128)S(1)}, s32[4,32]{1,0:T(4,128)}, u32[]{:S(2)}) copy-start(s32[4,32]{1,0:T(4,128)} %index_in.1) | copy-start | bytes 1540
  12.1 0.7 %copy-start.9 = (s32[32]{0:T(128)S(1)}, s32[32]{0:T(128)}, u32[]{:S(2)}) copy-start(s32[32]{0:T(128)} %param.27) | copy-start | bytes 388
  12.1 0.7 %copy-start.10 = (s32[16]{0:T(128)S(1)}, s32[16]{0:T(128)}, u32[]{:S(2)}) copy-start(s32[16]{0:T(128)} %source_elem.1) | copy-start | bytes 196
  18.3 6.7 %collective-permute-start.3 = (f32[16,256]{1,0:T(8,128)S(1)}, f32[16,256]{1,0:T(8,128)S(1)}, u32[]{:S(2)}, u32[]{:S(2)}) collective-permute-start(f32[16,256]{1,0:T(8,128)S(1)} %get-tuple-element.66), channel_id=1, source_target_pairs={{0,2},{2,4},{4,6},{6,8},{8,10},{10,12},{12,14},{14,16},{16,18},{18... | collective-permute-start | bytes 49160 | tf_op jit(solution)/shard_map/ppermute | solution.py:449
  18.4 6.6 %collective-permute-start.4 = (f32[16,256]{1,0:T(8,128)S(1)}, f32[16,256]{1,0:T(8,128)S(1)}, u32[]{:S(2)}, u32[]{:S(2)}) collective-permute-start(f32[16,256]{1,0:T(8,128)S(1)} %get-tuple-element.67), channel_id=1, source_target_pairs={{2,0},{4,2},{6,4},{8,6},{10,8},{12,10},{14,12},{16,14},{18,16},{20... | collective-permute-start | bytes 49160 | tf_op jit(solution)/shard_map/ppermute | solution.py:450
  22.8 3.7 %collective-permute-start.5 = (f32[16,256]{1,0:T(8,128)S(1)}, f32[16,256]{1,0:T(8,128)S(1)}, u32[]{:S(2)}, u32[]{:S(2)}) collective-permute-start(f32[16,256]{1,0:T(8,128)S(1)} %get-tuple-element.68), channel_id=1, source_target_pairs={{0,1},{1,0},{2,3},{3,2},{4,5},{5,4},{6,7},{7,6},{8,9},{9,8},{10,11... | collective-permute-start | bytes 49160 | tf_op jit(solution)/shard_map/ppermute | solution.py:448

commit v2 on v1

--- a/solution.py
+++ b/solution.py
@@ -161,26 +161,30 @@
     return lax.axis_index("off")
 
 
-def put_sends(rows, bw_ref, fw_ref, self_ref, off_refs):
-    bw_ref[...] = rows[0:16]
-    fw_ref[...] = rows[16:32]
+def turned_around():
+    return 16 - 16 * lax.rem(lax.axis_index("fault"), 2)
+
+
+def put_sends(rows, far_ref, chip_ref, self_ref, off_refs):
+    chip_ref[...] = rows[0:16]
+    far_ref[...] = rows[16:32]
     self_ref[...] = rows[32:48]
     for k, ref in enumerate(off_refs):
         ref[...] = rows[48 + 16 * k : 64 + 16 * k]
 
 
 def first_kernel(n_off, *refs):
-    sources = refs[:6]
-    landed = refs[-7:-1]
+    sources = refs[:10]
+    landed = refs[-7:-1] + refs[10:14]
     copies = [
         pltpu.make_async_copy(source, target, refs[-1].at[k])
         for k, (source, target) in enumerate(zip(sources, landed))
     ]
     for copy in copies:
         copy.start()
-    state_in, star_in, stiff_in, proj_in, elem_in, face_in = landed
-    refs = refs[6:-7]
-    (state_out, first_out, second_out, star_out, left_out, proj_out, tab_out, pick_out, bw, fw, own) = refs[:11]
+    state_in, star_in, stiff_in, proj_in, elem_in, face_in = landed[:6]
+    refs = refs[14:-7]
+    (state_out, first_out, second_out, star_out, left_out, proj_out, tab_out, pick_out, far, chip, own) = refs[:11]
     offs = refs[11 : 11 + n_off - 1]
     x_ref, y_ref, tall, slot_pad = refs[11 + n_off - 1 :]
     tall[...] = jnp.zeros((W, LANES), F32)
@@ -212,7 +216,7 @@
     block = row >> 4
     within = row & 15
     target = lax.rem(block - 2 + off_rank(), n_off)
-    slot = jnp.where(row < 32, row, jnp.where(within < SO, 32 + target * SO + within, -1))
+    slot = jnp.where(row < 32, row ^ turned_around(), jnp.where(within < SO, 32 + target * SO + within, -1))
     wanted = jnp.where(lane_iota(rows) == slot, slot_pad[0:1, :], 0)
     entry = jnp.sum(wanted.astype(F32), axis=1, keepdims=True)
     pick = jnp.where(lane_iota(rows).astype(F32) + 1.0 == entry, 1.0, 0.0).astype(BF16)
@@ -220,7 +224,7 @@
 
     predict(star_out, left_out, x_ref, y_ref, first_out, second_out)
     make_table(proj_out[...], first_out[...], tab_out)
-    put_sends(send_rows(pick, tab_out), bw, fw, own, offs)
+    put_sends(send_rows(pick, tab_out), far, chip, own, offs)
 
 
 def gather_local(pick, tab_ref):
@@ -303,7 +307,7 @@
     within = row & 15
     source = lax.rem(off_rank() + n_off + 2 - (row >> 4), n_off)
     place = jnp.where(
-        row < 32, LANES + row, jnp.where(within < SO, LANES + 32 + source * SO + within, -1)
+        row < 32, LANES + (row ^ turned_around()), jnp.where(within < SO, LANES + 32 + source * SO + within, -1)
     )
     pick_far_out[...] = jnp.where(place == index_row, 1.0, 0.0).astype(BF16)
     here_out[...] = gather_local(pick_here, tab)
@@ -312,11 +316,11 @@
         tall[q * SRC : q * SRC + SRC, 0:M] = source_in[q]
     origin = (lax.axis_index("fault") * n_off + off_rank()) * E
     row = row_iota(SRC)
-    goal = jnp.full((SRC, LANES), -1, jnp.int32)
-    for s in range(SRC):
-        goal = jnp.where(row == s, source_elem[s] - origin, goal)
+    ipad[0:1, 0:SRC] = source_elem[...] - origin
+    lane = lane_iota(SRC)
+    here = jnp.where(lane == row, ipad[0:1, :], 0).astype(F32)
+    goal = jnp.sum(here, axis=1, keepdims=True).astype(jnp.int32)
     y_ref[0 : Q * SRC, :] = jnp.zeros((Q * SRC, W), F32)
-    lane = lane_iota(SRC)
     for q in range(Q):
         lane_in = lane - 32 * (q % 4)
         hit = jnp.logical_and(lane_in == goal, jnp.logical_and(goal >= 0, goal < E))
@@ -333,9 +337,9 @@
     part_out[...] = product(left_out[...], y_ref[...])
 
 
-def arrive(fw, bw, own, offs, pick_far, stage):
-    stage[0:16, :] = fw[...]
-    stage[16:32, :] = bw[...]
+def arrive(chip, far, own, offs, pick_far, stage):
+    stage[0:16, :] = chip[...]
+    stage[16:32, :] = far[...]
     stage[32:48, :] = own[...]
     for k, ref in enumerate(offs):
         stage[48 + 16 * k : 64 + 16 * k, :] = ref[...]
@@ -373,14 +377,14 @@
 
 
 def middle_kernel(
-    n_off, state, second, part, here, fnbr, flags, lift, star, left, proj, pick, pick_far, own, fw, bw, *refs
+    n_off, state, second, part, here, fnbr, flags, lift, star, left, proj, pick, pick_far, own, chip, far, *refs
 ):
     offs = refs[: n_off - 1]
     outs = refs[n_off - 1 :]
-    near_out, half_out, later_out, tab_out, bw_out, fw_out, own_out = outs[:7]
+    near_out, half_out, later_out, tab_out, far_out, chip_out, own_out = outs[:7]
     off_outs = outs[7 : 7 + n_off - 1]
     x_ref, y_ref, stage, acc = outs[7 + n_off - 1 :]
-    near_out[...] = here[...] + arrive(fw, bw, own, offs, pick_far, stage)
+    near_out[...] = here[...] + arrive(chip, far, own, offs, pick_far, stage)
     total = part[...] + neighbour_flux(near_out, fnbr, flags, lift, y_ref)
     fine = jnp.concatenate([wide_fine(flags)] * 3, axis=1)
     base = state[...]
@@ -391,7 +395,7 @@
     later = jnp.where(fine, acc[...], second[...])
     later_out[...] = later
     make_table(proj[...], later, tab_out)
-    put_sends(send_rows(pick[...], tab_out), bw_out, fw_out, own_out, off_outs)
+    put_sends(send_rows(pick[...], tab_out), far_out, chip_out, own_out, off_outs)
 
 
 def late_side_kernel(
@@ -406,11 +410,11 @@
     here_out[...] = gather_local(pick_here[...], tab) + jnp.where(row, 0.0, near_first[...])
 
 
-def last_kernel(n_off, base, here, fnbr, flags, lift, pick_far, own, fw, bw, *refs):
+def last_kernel(n_off, base, here, fnbr, flags, lift, pick_far, own, chip, far, *refs):
     offs = refs[: n_off - 1]
     out, near, y_ref, stage, tall = refs[n_off - 1 :]
     tall[M:LANES, :] = jnp.zeros((LANES - M, W), F32)
-    near[...] = here[...] + arrive(fw, bw, own, offs, pick_far, stage)
+    near[...] = here[...] + arrive(chip, far, own, offs, pick_far, stage)
     total = base[...] + neighbour_flux(near, fnbr, flags, lift, y_ref)
     tall[0:M, :] = total
     turned = tall[...].T
@@ -440,15 +444,18 @@
     )(*ins)
 
 
-def trade(bw, fw, offs, n_fault, n_off):
-    up = [(i, (i + 1) % n_fault) for i in range(n_fault)]
-    down = [((i + 1) % n_fault, i) for i in range(n_fault)]
+def trade(far, chip, offs, n_fault, n_off):
+    def exchange(offset):
+        firsts = range(offset, n_fault, 2)
+        pairs = [(i, (i + 1) % n_fault) for i in firsts]
+        return pairs + [(j, i) for i, j in pairs]
+
     got = []
+    got_far = lax.ppermute(far, "fault", exchange(1))
+    got_chip = lax.ppermute(chip, "fault", exchange(0))
     for k, rows in enumerate(offs, 1):
         got.append(lax.ppermute(rows, "off", [(j, (j + k) % n_off) for j in range(n_off)]))
-    ahead = lax.ppermute(fw, "fault", up)
-    behind = lax.ppermute(bw, "fault", down)
-    return ahead, behind, got
+    return got_chip, got_far, got
 
 
 def on_device(
@@ -485,11 +492,16 @@
         jnp.transpose(face_proj, (2, 0, 1)),
         send_elem,
         send_face,
+        nbr_index,
+        orientation,
+        cluster.reshape(1, E),
+        source_elem.reshape(1, SRC),
     )
     outs = call(
         functools.partial(first_kernel, n_off),
         [pltpu.with_memory_space_constraint(x, pltpu.HBM) for x in given],
-        [
+        [shape(*x.shape, dtype=x.dtype) for x in given[6:]]
+        + [
             wide,
             wide,
             wide,
@@ -506,12 +518,14 @@
             vmem((W, LANES), F32),
             vmem((8, LANES), jnp.int32),
         ]
-        + [vmem(x.shape, x.dtype) for x in given]
+        + [vmem(x.shape, x.dtype) for x in given[:6]]
         + [pltpu.SemaphoreType.DMA((len(given),))],
         hbm=range(len(given)),
     )
-    state, first, second, star, left, proj, tab, pick, bw, fw, own = outs[:11]
-    got_fw, got_bw, got_off = trade(bw, fw, outs[11:], n_fault, n_off)
+    index, orient, fine, spots = outs[:4]
+    outs = outs[4:]
+    state, first, second, star, left, proj, tab, pick, far, chip, own = outs[:11]
+    got_chip, got_far, got_off = trade(far, chip, outs[11:], n_fault, n_off)
     part, coef, fnbr, left_all, lift, here, pick_here, pick_far, flags, source = call(
         functools.partial(side_kernel, n_off),
         (
@@ -524,10 +538,10 @@
             flux_minus,
             face_turn,
             jnp.transpose(face_lift, (1, 0, 2)),
-            nbr_index,
-            orientation,
-            cluster.reshape(1, E),
-            source_elem,
+            index,
+            orient,
+            fine,
+            spots,
             jnp.transpose(source_term, (1, 0, 2)),
         ),
         [
@@ -549,16 +563,15 @@
             vmem((LANES, LANES), F32),
             vmem((8, LANES), jnp.int32),
         ],
-        smem=(12,),
     )
     outs = call(
         functools.partial(middle_kernel, n_off),
-        (state, second, part, here, fnbr, flags, lift, star, left, proj, pick, pick_far, own, got_fw, got_bw, *got_off),
+        (state, second, part, here, fnbr, flags, lift, star, left, proj, pick, pick_far, own, got_chip, got_far, *got_off),
         [near, wide, wide, table] + [block] * (3 + n_off - 1),
         [vmem((M, W), F32), vmem((12 * JP, W), F32), vmem((rows, TAB), F32), vmem((M, W), F32)],
     )
-    near_first, half, later, tab, bw, fw, own = outs[:7]
-    got_fw, got_bw, got_off = trade(bw, fw, outs[7:], n_fault, n_off)
+    near_first, half, later, tab, far, chip, own = outs[:7]
+    got_chip, got_far, got_off = trade(far, chip, outs[7:], n_fault, n_off)
     base, here = call(
         late_side_kernel,
         (first, second, later, half, source, near_first, tab, coef, left_all, flags, pick_here),
@@ -567,7 +580,7 @@
     )
     (result,) = call(
         functools.partial(last_kernel, n_off),
-        (base, here, fnbr, flags, lift, pick_far, own, got_fw, got_bw, *got_off),
+        (base, here, fnbr, flags, lift, pick_far, own, got_chip, got_far, *got_off),
         [shape(Q, E, M)],
         [vmem((Q * JP + 8, LANES), F32), vmem((12 * JP, W), F32), vmem((rows, TAB), F32), vmem((LANES, W), F32)],
     )

time: 28.1 us -> 26 us (0.925)
  starting transfers between devices: 13.3 us -> 11.5 us
  waiting for transfers between devices: 1.56 us -> 2.52 us
  local copies, waits for them, and re-layouts: 0.64 us -> 0.03 us
  Pallas kernels: 12.3 us -> 11.7 us
    ppermute x4, starting transfers between devices: 10.1 us -> 8.51 us  [the longest x2 7.84 us: trade(): got_far = lax.ppermute(far, 'fault', exchange(1))]
    ppermute x4, waiting for transfers between devices: 0.01 us -> 1.44 us  [the longest x2 1.43 us: trade(): got_far = lax.ppermute(far, 'fault', exchange(1))]
    unnamed x22 -> x14, local copies, waits for them, and re-layouts: 0.64 us -> 0.03 us
    pallas_call x5, Pallas kernels: 12.3 us -> 11.7 us  [call(): pl.pallas_call(kernel, in_specs=specs, out_specs=[pl.BlockSpec(memory_spa...]
    ppermute x2, waiting for transfers between devices: 1.55 us -> 1.09 us  [trade(): lax.ppermute(rows, 'off', [(j, (j + k) % n_off) for j in range(n_off)])]
  transfers between devices with their start and end apart: 6 -> 6, of which waited for: 1 -> 2; matrix products, arithmetic and copies ran while one was open for 0% -> 0% of each run, Pallas kernels for 9% -> 7%
where the time goes in v2:
time: 26 us; the launch traced here: 25.9 us
  Pallas kernels  11.7 us (45%)
  starting transfers between devices  11.5 us (44%)
  waiting for transfers between devices  2.52 us (10%)
    pallas_call x5, Pallas kernels, call(): pl.pallas_call(kernel, in_specs=specs, out_specs=[pl.BlockSpec(memory_spa...  11.7 us
    ppermute x2, starting transfers between devices, trade(): got_far = lax.ppermute(far, 'fault', exchange(1))  7.84 us
    ppermute x2, starting transfers between devices, trade(): lax.ppermute(rows, 'off', [(j, (j + k) % n_off) for j in range(n_off)])  2.98 us
    ppermute x2, waiting for transfers between devices, trade(): got_far = lax.ppermute(far, 'fault', exchange(1))  1.43 us
    ppermute x2, waiting for transfers between devices, trade(): lax.ppermute(rows, 'off', [(j, (j + k) % n_off) for j in range(n_off)])  1.09 us
    ppermute x2, starting transfers between devices, trade(): got_chip = lax.ppermute(chip, 'fault', exchange(0))  0.67 us
  transfers between devices with their start and end apart: 6, of which 2 were waited for; matrix products, arithmetic and copies ran while one was open for 0% of the time, Pallas kernels for 7%

profile of v2, /device:TPU:0, one launch (start us, length us, event | category | flops | bytes accessed | tf_op | source)
XLA Modules:
  0.0 25.9 jit_solution(7335313099146113133)
XLA Ops:
  0.0 0.0 copy-start
  0.0 0.0 copy-start.1
  0.0 0.0 copy-start.2
  0.0 0.0 copy-start.3
  0.0 0.0 copy-start.4
  0.0 0.0 copy-start.5
  0.0 0.0 copy-start.6
  0.0 4.6 %shard_map.163 = (s32[4,32]{1,0:T(4,128)S(1)}, s32[4,32]{1,0:T(4,128)S(1)}, s32[1,32]{1,0:T(1,128)S(1)}, s32[1,16]{1,0:T(1,128)S(1)}, f32[56,384]{1,0:T(8,128)S(...) custom-call(f32[9,32,56]{2,1,0:T(8,128)} %bitcast.15, ...), custom_call_target="tpu_custom_call" | custom-call | flops 2000000000 | bytes 2000000 | tf_op jit(solution)/shard_map/pallas_call | solution.py:436
  4.6 0.6 %collective-permute-start = (f32[16,256]{1,0:T(8,128)S(1)}, f32[16,256]{1,0:T(8,128)S(1)}, u32[]{:S(2)}, u32[]{:S(2)}) collective-permute-start(f32[16,256]{1,0:T(8,128)S(1)} %get-tuple-element.60), channel_id=1, source_target_pairs={{0,2},{4,6},{8,10},{12,14},{16,18},{20,22},{24,26},{28,30},{2,0},{... | collective-permute-start | bytes 49160 | tf_op jit(solution)/shard_map/ppermute | solution.py:455
  5.2 5.7 %collective-permute-start.1 = (f32[16,256]{1,0:T(8,128)S(1)}, f32[16,256]{1,0:T(8,128)S(1)}, u32[]{:S(2)}, u32[]{:S(2)}) collective-permute-start(f32[16,256]{1,0:T(8,128)S(1)} %get-tuple-element.61), channel_id=1, source_target_pairs={{2,4},{6,8},{10,12},{14,16},{18,20},{22,24},{26,28},{30,0},{4,2},{... | collective-permute-start | bytes 49160 | tf_op jit(solution)/shard_map/ppermute | solution.py:454
  10.9 1.5 %collective-permute-start.2 = (f32[16,256]{1,0:T(8,128)S(1)}, f32[16,256]{1,0:T(8,128)S(1)}, u32[]{:S(2)}, u32[]{:S(2)}) collective-permute-start(f32[16,256]{1,0:T(8,128)S(1)} %get-tuple-element.62), channel_id=1, source_target_pairs={{0,1},{1,0},{2,3},{3,2},{4,5},{5,4},{6,7},{7,6},{8,9},{9,8},{10,11... | collective-permute-start | bytes 49160 | tf_op jit(solution)/shard_map/ppermute | solution.py:457
  12.3 0.0 copy-done
  12.4 0.0 copy-done.1
  12.4 0.0 copy-done.2
  12.4 0.0 copy-done.3
  12.4 0.0 copy-done.4
  12.4 0.0 copy-done.5
  12.4 0.0 copy-done.6
  12.4 1.1 %shard_map.164 = (f32[56,384]{1,0:T(8,128)S(1)}, f32[112,384]{1,0:T(8,128)S(1)}, f32[144,128]{1,0:T(8,128)S(1)}, bf16[112,400]{1,0:T(8,128)(2,1)S(1)}, bf16[112,...) custom-call(f32[56,384]{1,0:T(8,128)S(1)} %get-tuple-element.41.firs, ...), custom_call_target="tpu_custom_call" | custom-call | flops 2000000000 | bytes 2000000 | tf_op jit(solution)/shard_map/pallas_call | solution.py:436
  13.5 0.0 collective-permute-done.chip
  13.5 0.0 collective-permute-done.1.far
  13.5 1.1 %collective-permute-done.2.refs_0_ = f32[16,256]{1,0:T(8,128)S(1)} collective-permute-done((f32[16,256]{1,0:T(8,128)S(1)}, f32[16,256]{1,0:T(8,128)S(1)}, u32[]{:S(2)}, u32[]{:S(2)}) %collective-permute-start.2) | collective-permute-done | bytes 16416 | tf_op jit(solution)/shard_map/ppermute | solution.py:457
  14.6 3.8 %shard_map.165 = (f32[224,128]{1,0:T(8,128)S(1)}, f32[56,384]{1,0:T(8,128)S(1)}, f32[56,384]{1,0:T(8,128)S(1)}, f32[256,128]{1,0:T(8,128)S(1)}, f32[16,256]{1,0:...) custom-call(f32[56,384]{1,0:T(8,128)S(1)} %get-tuple-element.43.state, ...), custom_call_target="tpu_custom_call" | custom-call | flops 2000000000 | bytes 2000000 | tf_op jit(solution)/shard_map/pallas_call | solution.py:436
  18.4 0.1 collective-permute-start.3
  18.5 2.2 %collective-permute-start.4 = (f32[16,256]{1,0:T(8,128)S(1)}, f32[16,256]{1,0:T(8,128)S(1)}, u32[]{:S(2)}, u32[]{:S(2)}) collective-permute-start(f32[16,256]{1,0:T(8,128)S(1)} %get-tuple-element.75), channel_id=1, source_target_pairs={{2,4},{6,8},{10,12},{14,16},{18,20},{22,24},{26,28},{30,0},{4,2},{... | collective-permute-start | bytes 49160 | tf_op jit(solution)/shard_map/ppermute | solution.py:454
  20.7 1.5 %collective-permute-start.5 = (f32[16,256]{1,0:T(8,128)S(1)}, f32[16,256]{1,0:T(8,128)S(1)}, u32[]{:S(2)}, u32[]{:S(2)}) collective-permute-start(f32[16,256]{1,0:T(8,128)S(1)} %get-tuple-element.76), channel_id=1, source_target_pairs={{0,1},{1,0},{2,3},{3,2},{4,5},{5,4},{6,7},{7,6},{8,9},{9,8},{10,11... | collective-permute-start | bytes 49160 | tf_op jit(solution)/shard_map/ppermute | solution.py:457
  22.2 0.8 %shard_map.166 = (f32[56,384]{1,0:T(8,128)S(1)}, f32[224,128]{1,0:T(8,128)S(1)}) custom-call(f32[56,384]{1,0:T(8,128)S(1)} %get-tuple-element.41.first_in.first, f32[56,384]{1,0:T(8,128)S(1)} %get-tuple-element.42.second, f32[56,384]{1,0:T(8,128)S(1)} %get-tuple-element.63.later, f32[56,384]{1,0:T(8,128)S(1)} %get-tuple-element.64.half, ...), custom_call_target="tpu_custom_call" | custom-call | flops 2000000000 | bytes 2000000 | tf_op jit(solution)/shard_map/pallas_call | solution.py:436
  23.0 0.0 collective-permute-done.3.chip
  23.0 1.4 %collective-permute-done.4.far = f32[16,256]{1,0:T(8,128)S(1)} collective-permute-done((f32[16,256]{1,0:T(8,128)S(1)}, f32[16,256]{1,0:T(8,128)S(1)}, u32[]{:S(2)}, u32[]{:S(2)}) %collective-permute-start.4) | collective-permute-done | bytes 16416 | tf_op jit(solution)/shard_map/ppermute | solution.py:454
  24.4 0.0 collective-permute-done.5.refs_0_
  24.4 1.5 %shard_map.167 = f32[9,32,56]{2,1,0:T(8,128)} custom-call(f32[56,384]{1,0:T(8,128)S(1)} %get-tuple-element.71.base, f32[224,128]{1,0:T(8,128)S(1)} %get-tuple-element.72.here, f32[144,128]{1,0:T(8,128)S(1)} %get-tuple-element.52.fnbr, s32[8,128]{1,0:T(8,128)S(1)} %get-tuple-element.53.flags, bf16[112,288]{1,0:T(8,128)(2,1)S(1)} %get-tuple-element.54.lift, ...), custom_call_target="tpu_custom_call" | custom-call | flops 2000000000 | bytes 2000000 | tf_op jit(solution)/shard_map/pallas_call | solution.py:436
Async XLA Ops:
  0.0 12.4 %copy-start = (f32[4,9,9,32]{3,0,2,1:T(4,128)S(1)}, f32[4,9,9,32]{3,0,2,1:T(4,128)}, u32[]{:S(2)}) copy-start(f32[4,9,9,32]{3,0,2,1:T(4,128)} %param.19) | copy-start | bytes 124420
  0.0 12.4 %copy-start.1 = (f32[4,9,9,32]{3,0,2,1:T(4,128)S(1)}, f32[4,9,9,32]{3,0,2,1:T(4,128)}, u32[]{:S(2)}) copy-start(f32[4,9,9,32]{3,0,2,1:T(4,128)} %param.20) | copy-start | bytes 124420
  0.0 12.4 %copy-start.2 = (f32[4,56,56]{2,1,0:T(8,128)S(1)}, f32[4,56,56]{2,1,0:T(8,128)}, u32[]{:S(2)}) copy-start(f32[4,56,56]{2,1,0:T(8,128)} %minus_in.1) | copy-start | bytes 150532
  0.0 12.4 %copy-start.3 = (f32[3,56,56]{2,1,0:T(8,128)S(1)}, f32[3,56,56]{2,1,0:T(8,128)}, u32[]{:S(2)}) copy-start(f32[3,56,56]{2,1,0:T(8,128)} %vol_in.1) | copy-start | bytes 112900
  0.0 12.4 %copy-start.4 = (f32[16,9,56]{2,0,1:T(8,128)S(1)}, f32[16,9,56]{2,0,1:T(8,128)}, u32[]{:S(2)}) copy-start(f32[16,9,56]{2,0,1:T(8,128)} %param.33) | copy-start | bytes 96772
  0.0 12.4 %copy-start.5 = (f32[4,21,56]{2,0,1:T(4,128)S(1)}, f32[4,21,56]{2,0,1:T(4,128)}, u32[]{:S(2)}) copy-start(f32[4,21,56]{2,0,1:T(4,128)} %param.26) | copy-start | bytes 56452
  0.0 12.4 %copy-start.6 = (f32[3,21,21]{2,1,0:T(8,128)S(1)}, f32[3,21,21]{2,1,0:T(8,128)}, u32[]{:S(2)}) copy-start(f32[3,21,21]{2,1,0:T(8,128)} %turn_in.1) | copy-start | bytes 15880
  4.6 8.9 %collective-permute-start = (f32[16,256]{1,0:T(8,128)S(1)}, f32[16,256]{1,0:T(8,128)S(1)}, u32[]{:S(2)}, u32[]{:S(2)}) collective-permute-start(f32[16,256]{1,0:T(8,128)S(1)} %get-tuple-element.60), channel_id=1, source_target_pairs={{0,2},{4,6},{8,10},{12,14},{16,18},{20,22},{24,26},{28,30},{2,0},{... | collective-permute-start | bytes 49160 | tf_op jit(solution)/shard_map/ppermute | solution.py:455
  5.2 8.3 %collective-permute-start.1 = (f32[16,256]{1,0:T(8,128)S(1)}, f32[16,256]{1,0:T(8,128)S(1)}, u32[]{:S(2)}, u32[]{:S(2)}) collective-permute-start(f32[16,256]{1,0:T(8,128)S(1)} %get-tuple-element.61), channel_id=1, source_target_pairs={{2,4},{6,8},{10,12},{14,16},{18,20},{22,24},{26,28},{30,0},{4,2},{... | collective-permute-start | bytes 49160 | tf_op jit(solution)/shard_map/ppermute | solution.py:454
  10.9 3.7 %collective-permute-start.2 = (f32[16,256]{1,0:T(8,128)S(1)}, f32[16,256]{1,0:T(8,128)S(1)}, u32[]{:S(2)}, u32[]{:S(2)}) collective-permute-start(f32[16,256]{1,0:T(8,128)S(1)} %get-tuple-element.62), channel_id=1, source_target_pairs={{0,1},{1,0},{2,3},{3,2},{4,5},{5,4},{6,7},{7,6},{8,9},{9,8},{10,11... | collective-permute-start | bytes 49160 | tf_op jit(solution)/shard_map/ppermute | solution.py:457
  18.4 4.6 %collective-permute-start.3 = (f32[16,256]{1,0:T(8,128)S(1)}, f32[16,256]{1,0:T(8,128)S(1)}, u32[]{:S(2)}, u32[]{:S(2)}) collective-permute-start(f32[16,256]{1,0:T(8,128)S(1)} %get-tuple-element.74), channel_id=1, source_target_pairs={{0,2},{4,6},{8,10},{12,14},{16,18},{20,22},{24,26},{28,30},{2,0},{... | collective-permute-start | bytes 49160 | tf_op jit(solution)/shard_map/ppermute | solution.py:455
  18.5 5.9 %collective-permute-start.4 = (f32[16,256]{1,0:T(8,128)S(1)}, f32[16,256]{1,0:T(8,128)S(1)}, u32[]{:S(2)}, u32[]{:S(2)}) collective-permute-start(f32[16,256]{1,0:T(8,128)S(1)} %get-tuple-element.75), channel_id=1, source_target_pairs={{2,4},{6,8},{10,12},{14,16},{18,20},{22,24},{26,28},{30,0},{4,2},{... | collective-permute-start | bytes 49160 | tf_op jit(solution)/shard_map/ppermute | solution.py:454
  20.7 3.7 %collective-permute-start.5 = (f32[16,256]{1,0:T(8,128)S(1)}, f32[16,256]{1,0:T(8,128)S(1)}, u32[]{:S(2)}, u32[]{:S(2)}) collective-permute-start(f32[16,256]{1,0:T(8,128)S(1)} %get-tuple-element.76), channel_id=1, source_target_pairs={{0,1},{1,0},{2,3},{3,2},{4,5},{5,4},{6,7},{7,6},{8,9},{9,8},{10,11... | collective-permute-start | bytes 49160 | tf_op jit(solution)/shard_map/ppermute | solution.py:457

commit v3 on v2

--- a/solution.py
+++ b/solution.py
@@ -96,6 +96,15 @@
     return out
 
 
+def place_rows(source, target, start, members):
+    for d in members:
+        for c in range(2):
+            target[start + d * 16 : start + d * 16 + Q, c * 128 : c * 128 + 128] = group_place(
+                [source[q, :, d, :] for q in range(4 * c, 4 * c + 4)]
+            )
+    target[start : start + Q, 256:W] = group_place([source[Q - 1, :, d, :] for d in members])
+
+
 def group_place(parts):
     if len(parts) < 4:
         parts = parts + [jnp.zeros((parts[0].shape[0], E * (4 - len(parts))), parts[0].dtype)]
@@ -105,13 +114,23 @@
 def weigh(rows_of, x_ref, y_ref, count):
     for tile in range(M // 8):
         spans = spread([x_ref[tile * 8 : tile * 8 + 8, c * 128 : c * 128 + 128] for c in range(3)])
+
+        def mixed(row, column):
+            total = rows_of[row : row + 1, column : column + 128] * spans[0]
+            for p in range(1, Q):
+                total = total + rows_of[row + p : row + p + 1, column : column + 128] * spans[p]
+            return total
+
         for d in range(count):
-            for c in range(3):
-                total = rows_of[d * 16 : d * 16 + 1, c * 128 : c * 128 + 128] * spans[0]
-                for p in range(1, Q):
-                    total = total + rows_of[d * 16 + p : d * 16 + p + 1, c * 128 : c * 128 + 128] * spans[p]
+            start = d * M + tile * 8
+            for c in range(2):
+                y_ref[start : start + 8, c * 128 : c * 128 + 128] = mixed(d * 16, c * 128)
+        for pack in range(0, count, 4):
+            total = mixed(pack * 16, 256)
+            for d in range(pack, min(pack + 4, count)):
                 start = d * M + tile * 8
-                y_ref[start : start + 8, c * 128 : c * 128 + 128] = total
+                moved = roll(total, 128 - 32 * (d - pack)) if d > pack else total
+                y_ref[start : start + 8, 256:W] = moved
 
 
 def predict(star, left, x_ref, y_ref, first_ref, second_ref):
@@ -120,26 +139,18 @@
     first_ref[...] = EARLY[0] * state
     if second_ref is not None:
         second_ref[...] = LATE[0] * state
-
-    def step(k, carry):
+    for k in range(1, TERMS):
         weigh(star, x_ref, y_ref, 3)
         result = product(left[...], y_ref[0 : 3 * M + 8, :])
         x_ref[...] = result
-        early = jnp.float32(EARLY[1])
-        late = jnp.float32(LATE[1])
-        for degree in range(2, TERMS):
-            early = jnp.where(k == degree, EARLY[degree], early)
-            late = jnp.where(k == degree, LATE[degree], late)
-        first_ref[...] = first_ref[...] + early * result
+        first_ref[...] = first_ref[...] + EARLY[k] * result
         if second_ref is not None:
-            second_ref[...] = second_ref[...] + late * result
-        return carry
-
-    lax.fori_loop(1, TERMS, step, 0)
+            second_ref[...] = second_ref[...] + LATE[k] * result
 
 
 def make_table(project, x, tab_ref):
-    faced = product(project, x)
+    high = x.astype(BF16).astype(F32)
+    faced = dot(project, jnp.concatenate([high, high, x - high], axis=0).astype(BF16))
     for tile in range(3):
         for c in range(3):
             parts = [
@@ -196,11 +207,8 @@
     state = tall[...].T[0:M, :]
     x_ref[...] = state
     state_out[...] = state
-    for d in range(3):
-        for c in range(3):
-            star_out[d * 16 : d * 16 + Q, c * 128 : c * 128 + 128] = group_place(
-                [star_in[q, :, d, :] for q in range(4 * c, min(4 * c + 4, Q))]
-            )
+    star_out[...] = jnp.zeros((48, W), F32)
+    place_rows(star_in, star_out, 0, range(3))
     tall[...] = jnp.zeros((W, LANES), F32)
     for d in range(3):
         tall[d * M : d * M + M, 0:M] = stiff_in[d]
@@ -208,7 +216,10 @@
     tall[0 : 4 * JP, :] = jnp.zeros((4 * JP, LANES), F32)
     for f in range(4):
         tall[f * JP : f * JP + J, 0:M] = proj_in[:, f, :]
-    proj_out[...] = stack_split(tall[0 : 4 * JP, 0:M])
+    values = tall[0 : 4 * JP, :].T[0:M]
+    high = values.astype(BF16).astype(F32)
+    stacked = jnp.concatenate([high, values - high, high, jnp.zeros((LANES * 2 - 3 * M, 4 * JP), F32)], axis=0)
+    proj_out[...] = stacked.T[:, 0 : 3 * M].astype(BF16)
     slots = elem_in.shape[2]
     slot_pad[0:1, 0:slots] = face_in[0] * E + elem_in[0] + 1
     rows = 32 + 16 * n_off
@@ -264,19 +275,16 @@
     lift_pad,
     ipad,
 ):
-    coef_out[0:48, :] = star[...]
-    for f in range(4):
-        for c in range(3):
-            coef_out[(3 + f) * 16 : (3 + f) * 16 + Q, c * 128 : c * 128 + 128] = group_place(
-                [local_in[q, :, f, :] for q in range(4 * c, min(4 * c + 4, Q))]
-            )
+    coef_out[...] = jnp.zeros((7 * 16, W), F32)
+    place_rows(local_in, coef_out, 0, range(4))
+    coef_out[4 * 16 : 7 * 16, :] = star[...]
     for q in range(Q):
         fnbr_out[q * 16 : q * 16 + Q, :] = group_place([nbr_in[q, :, f, :] for f in range(4)])
     tall[...] = jnp.zeros((512, LANES), F32)
+    for f in range(4):
+        tall[f * M : f * M + M, 0:M] = minus_in[f]
     for d in range(3):
-        tall[d * M : d * M + M, 0:M] = vol_in[d]
-    for f in range(4):
-        tall[(3 + f) * M : (4 + f) * M, 0:M] = minus_in[f]
+        tall[(4 + d) * M : (5 + d) * M, 0:M] = vol_in[d]
     left_out[...] = stack_split(tall[...].T[0:M, 0 : 7 * M + 8])
     turn_pad[...] = jnp.zeros((3 * JP, LANES), F32)
     for o in range(3):
@@ -507,7 +515,7 @@
             wide,
             shape(48, W),
             shape(2 * M, 3 * M + 8, dtype=BF16),
-            shape(8 * JP, M, dtype=BF16),
+            shape(4 * JP, 3 * M, dtype=BF16),
             table,
             shape(rows, LANES, dtype=BF16),
         ]

time: 26 us -> 25.1 us (0.965)
  Pallas kernels: 11.7 us -> 10.7 us
    pallas_call x5, Pallas kernels: 11.7 us -> 10.7 us  [call(): pl.pallas_call(kernel, in_specs=specs, out_specs=[pl.BlockSpec(memory_spa...]
where the time goes in v3:
time: 25.1 us; the launch traced here: 25 us
  starting transfers between devices  11.5 us (46%)
  Pallas kernels  10.7 us (43%)
  waiting for transfers between devices  2.68 us (11%)
    pallas_call x5, Pallas kernels, call(): pl.pallas_call(kernel, in_specs=specs, out_specs=[pl.BlockSpec(memory_spa...  10.7 us
    ppermute x2, starting transfers between devices, trade(): got_far = lax.ppermute(far, 'fault', exchange(1))  7.85 us
    ppermute x2, starting transfers between devices, trade(): lax.ppermute(rows, 'off', [(j, (j + k) % n_off) for j in range(n_off)])  2.98 us
    ppermute x2, waiting for transfers between devices, trade(): got_far = lax.ppermute(far, 'fault', exchange(1))  1.51 us
    ppermute x2, waiting for transfers between devices, trade(): lax.ppermute(rows, 'off', [(j, (j + k) % n_off) for j in range(n_off)])  1.17 us
    ppermute x2, starting transfers between devices, trade(): got_chip = lax.ppermute(chip, 'fault', exchange(0))  0.67 us
  transfers between devices with their start and end apart: 6, of which 2 were waited for; matrix products, arithmetic and copies ran while one was open for 0% of the time, Pallas kernels for 7%

profile of v3, /device:TPU:0, one launch (start us, length us, event | category | flops | bytes accessed | tf_op | source)
XLA Modules:
  0.0 25.0 jit_solution(7307372289717884789)
XLA Ops:
  0.0 0.0 copy-start
  0.0 0.0 copy-start.1
  0.0 0.0 copy-start.2
  0.0 0.0 copy-start.3
  0.0 0.0 copy-start.4
  0.0 0.0 copy-start.5
  0.0 0.0 copy-start.6
  0.0 4.1 %shard_map.163 = (s32[4,32]{1,0:T(4,128)S(1)}, s32[4,32]{1,0:T(4,128)S(1)}, s32[1,32]{1,0:T(1,128)S(1)}, s32[1,16]{1,0:T(1,128)S(1)}, f32[56,384]{1,0:T(8,128)S(...) custom-call(f32[9,32,56]{2,1,0:T(8,128)} %bitcast.15, ...), custom_call_target="tpu_custom_call" | custom-call | flops 2000000000 | bytes 2000000 | tf_op jit(solution)/shard_map/pallas_call | solution.py:444
  4.1 0.6 %collective-permute-start = (f32[16,256]{1,0:T(8,128)S(1)}, f32[16,256]{1,0:T(8,128)S(1)}, u32[]{:S(2)}, u32[]{:S(2)}) collective-permute-start(f32[16,256]{1,0:T(8,128)S(1)} %get-tuple-element.60), channel_id=1, source_target_pairs={{0,2},{4,6},{8,10},{12,14},{16,18},{20,22},{24,26},{28,30},{2,0},{... | collective-permute-start | bytes 49160 | tf_op jit(solution)/shard_map/ppermute | solution.py:463
  4.7 5.7 %collective-permute-start.1 = (f32[16,256]{1,0:T(8,128)S(1)}, f32[16,256]{1,0:T(8,128)S(1)}, u32[]{:S(2)}, u32[]{:S(2)}) collective-permute-start(f32[16,256]{1,0:T(8,128)S(1)} %get-tuple-element.61), channel_id=1, source_target_pairs={{2,4},{6,8},{10,12},{14,16},{18,20},{22,24},{26,28},{30,0},{4,2},{... | collective-permute-start | bytes 49160 | tf_op jit(solution)/shard_map/ppermute | solution.py:462
  10.4 1.5 %collective-permute-start.2 = (f32[16,256]{1,0:T(8,128)S(1)}, f32[16,256]{1,0:T(8,128)S(1)}, u32[]{:S(2)}, u32[]{:S(2)}) collective-permute-start(f32[16,256]{1,0:T(8,128)S(1)} %get-tuple-element.62), channel_id=1, source_target_pairs={{0,1},{1,0},{2,3},{3,2},{4,5},{5,4},{6,7},{7,6},{8,9},{9,8},{10,11... | collective-permute-start | bytes 49160 | tf_op jit(solution)/shard_map/ppermute | solution.py:465
  11.9 0.0 copy-done
  11.9 0.0 copy-done.1
  11.9 0.0 copy-done.2
  11.9 0.0 copy-done.3
  11.9 0.0 copy-done.4
  11.9 0.0 copy-done.5
  11.9 0.0 copy-done.6
  11.9 1.0 %shard_map.164 = (f32[56,384]{1,0:T(8,128)S(1)}, f32[112,384]{1,0:T(8,128)S(1)}, f32[144,128]{1,0:T(8,128)S(1)}, bf16[112,400]{1,0:T(8,128)(2,1)S(1)}, bf16[112,...) custom-call(f32[56,384]{1,0:T(8,128)S(1)} %get-tuple-element.41.firs, ...), custom_call_target="tpu_custom_call" | custom-call | flops 2000000000 | bytes 2000000 | tf_op jit(solution)/shard_map/pallas_call | solution.py:444
  12.9 0.0 collective-permute-done.chip
  12.9 0.0 collective-permute-done.1.far
  12.9 1.2 %collective-permute-done.2.refs_0_ = f32[16,256]{1,0:T(8,128)S(1)} collective-permute-done((f32[16,256]{1,0:T(8,128)S(1)}, f32[16,256]{1,0:T(8,128)S(1)}, u32[]{:S(2)}, u32[]{:S(2)}) %collective-permute-start.2) | collective-permute-done | bytes 16416 | tf_op jit(solution)/shard_map/ppermute | solution.py:465
  14.1 3.4 %shard_map.165 = (f32[224,128]{1,0:T(8,128)S(1)}, f32[56,384]{1,0:T(8,128)S(1)}, f32[56,384]{1,0:T(8,128)S(1)}, f32[256,128]{1,0:T(8,128)S(1)}, f32[16,256]{1,0:...) custom-call(f32[56,384]{1,0:T(8,128)S(1)} %get-tuple-element.43.state, ...), custom_call_target="tpu_custom_call" | custom-call | flops 2000000000 | bytes 2000000 | tf_op jit(solution)/shard_map/pallas_call | solution.py:444
  17.5 0.1 collective-permute-start.3
  17.6 2.2 %collective-permute-start.4 = (f32[16,256]{1,0:T(8,128)S(1)}, f32[16,256]{1,0:T(8,128)S(1)}, u32[]{:S(2)}, u32[]{:S(2)}) collective-permute-start(f32[16,256]{1,0:T(8,128)S(1)} %get-tuple-element.75), channel_id=1, source_target_pairs={{2,4},{6,8},{10,12},{14,16},{18,20},{22,24},{26,28},{30,0},{4,2},{... | collective-permute-start | bytes 49160 | tf_op jit(solution)/shard_map/ppermute | solution.py:462
  19.8 1.5 %collective-permute-start.5 = (f32[16,256]{1,0:T(8,128)S(1)}, f32[16,256]{1,0:T(8,128)S(1)}, u32[]{:S(2)}, u32[]{:S(2)}) collective-permute-start(f32[16,256]{1,0:T(8,128)S(1)} %get-tuple-element.76), channel_id=1, source_target_pairs={{0,1},{1,0},{2,3},{3,2},{4,5},{5,4},{6,7},{7,6},{8,9},{9,8},{10,11... | collective-permute-start | bytes 49160 | tf_op jit(solution)/shard_map/ppermute | solution.py:465
  21.3 0.7 %shard_map.166 = (f32[56,384]{1,0:T(8,128)S(1)}, f32[224,128]{1,0:T(8,128)S(1)}) custom-call(f32[56,384]{1,0:T(8,128)S(1)} %get-tuple-element.41.first_in.first, f32[56,384]{1,0:T(8,128)S(1)} %get-tuple-element.42.second, f32[56,384]{1,0:T(8,128)S(1)} %get-tuple-element.63.later, f32[56,384]{1,0:T(8,128)S(1)} %get-tuple-element.64.half, ...), custom_call_target="tpu_custom_call" | custom-call | flops 2000000000 | bytes 2000000 | tf_op jit(solution)/shard_map/pallas_call | solution.py:444
  22.0 0.0 collective-permute-done.3.chip
  22.0 1.5 %collective-permute-done.4.far = f32[16,256]{1,0:T(8,128)S(1)} collective-permute-done((f32[16,256]{1,0:T(8,128)S(1)}, f32[16,256]{1,0:T(8,128)S(1)}, u32[]{:S(2)}, u32[]{:S(2)}) %collective-permute-start.4) | collective-permute-done | bytes 16416 | tf_op jit(solution)/shard_map/ppermute | solution.py:462
  23.5 0.0 collective-permute-done.5.refs_0_
  23.5 1.5 %shard_map.167 = f32[9,32,56]{2,1,0:T(8,128)} custom-call(f32[56,384]{1,0:T(8,128)S(1)} %get-tuple-element.71.base, f32[224,128]{1,0:T(8,128)S(1)} %get-tuple-element.72.here, f32[144,128]{1,0:T(8,128)S(1)} %get-tuple-element.52.fnbr, s32[8,128]{1,0:T(8,128)S(1)} %get-tuple-element.53.flags, bf16[112,288]{1,0:T(8,128)(2,1)S(1)} %get-tuple-element.54.lift, ...), custom_call_target="tpu_custom_call" | custom-call | flops 2000000000 | bytes 2000000 | tf_op jit(solution)/shard_map/pallas_call | solution.py:444
Async XLA Ops:
  0.0 11.9 %copy-start = (f32[4,9,9,32]{3,0,2,1:T(4,128)S(1)}, f32[4,9,9,32]{3,0,2,1:T(4,128)}, u32[]{:S(2)}) copy-start(f32[4,9,9,32]{3,0,2,1:T(4,128)} %param.19) | copy-start | bytes 124420
  0.0 11.9 %copy-start.1 = (f32[4,9,9,32]{3,0,2,1:T(4,128)S(1)}, f32[4,9,9,32]{3,0,2,1:T(4,128)}, u32[]{:S(2)}) copy-start(f32[4,9,9,32]{3,0,2,1:T(4,128)} %param.20) | copy-start | bytes 124420
  0.0 11.9 %copy-start.2 = (f32[4,56,56]{2,1,0:T(8,128)S(1)}, f32[4,56,56]{2,1,0:T(8,128)}, u32[]{:S(2)}) copy-start(f32[4,56,56]{2,1,0:T(8,128)} %minus_in.1) | copy-start | bytes 150532
  0.0 11.9 %copy-start.3 = (f32[3,56,56]{2,1,0:T(8,128)S(1)}, f32[3,56,56]{2,1,0:T(8,128)}, u32[]{:S(2)}) copy-start(f32[3,56,56]{2,1,0:T(8,128)} %vol_in.1) | copy-start | bytes 112900
  0.0 11.9 %copy-start.4 = (f32[16,9,56]{2,0,1:T(8,128)S(1)}, f32[16,9,56]{2,0,1:T(8,128)}, u32[]{:S(2)}) copy-start(f32[16,9,56]{2,0,1:T(8,128)} %param.33) | copy-start | bytes 96772
  0.0 11.9 %copy-start.5 = (f32[4,21,56]{2,0,1:T(4,128)S(1)}, f32[4,21,56]{2,0,1:T(4,128)}, u32[]{:S(2)}) copy-start(f32[4,21,56]{2,0,1:T(4,128)} %param.26) | copy-start | bytes 56452
  0.0 11.9 %copy-start.6 = (f32[3,21,21]{2,1,0:T(8,128)S(1)}, f32[3,21,21]{2,1,0:T(8,128)}, u32[]{:S(2)}) copy-start(f32[3,21,21]{2,1,0:T(8,128)} %turn_in.1) | copy-start | bytes 15880
  4.1 8.8 %collective-permute-start = (f32[16,256]{1,0:T(8,128)S(1)}, f32[16,256]{1,0:T(8,128)S(1)}, u32[]{:S(2)}, u32[]{:S(2)}) collective-permute-start(f32[16,256]{1,0:T(8,128)S(1)} %get-tuple-element.60), channel_id=1, source_target_pairs={{0,2},{4,6},{8,10},{12,14},{16,18},{20,22},{24,26},{28,30},{2,0},{... | collective-permute-start | bytes 49160 | tf_op jit(solution)/shard_map/ppermute | solution.py:463
  4.7 8.2 %collective-permute-start.1 = (f32[16,256]{1,0:T(8,128)S(1)}, f32[16,256]{1,0:T(8,128)S(1)}, u32[]{:S(2)}, u32[]{:S(2)}) collective-permute-start(f32[16,256]{1,0:T(8,128)S(1)} %get-tuple-element.61), channel_id=1, source_target_pairs={{2,4},{6,8},{10,12},{14,16},{18,20},{22,24},{26,28},{30,0},{4,2},{... | collective-permute-start | bytes 49160 | tf_op jit(solution)/shard_map/ppermute | solution.py:462
  10.4 3.7 %collective-permute-start.2 = (f32[16,256]{1,0:T(8,128)S(1)}, f32[16,256]{1,0:T(8,128)S(1)}, u32[]{:S(2)}, u32[]{:S(2)}) collective-permute-start(f32[16,256]{1,0:T(8,128)S(1)} %get-tuple-element.62), channel_id=1, source_target_pairs={{0,1},{1,0},{2,3},{3,2},{4,5},{5,4},{6,7},{7,6},{8,9},{9,8},{10,11... | collective-permute-start | bytes 49160 | tf_op jit(solution)/shard_map/ppermute | solution.py:465
  17.5 4.5 %collective-permute-start.3 = (f32[16,256]{1,0:T(8,128)S(1)}, f32[16,256]{1,0:T(8,128)S(1)}, u32[]{:S(2)}, u32[]{:S(2)}) collective-permute-start(f32[16,256]{1,0:T(8,128)S(1)} %get-tuple-element.74), channel_id=1, source_target_pairs={{0,2},{4,6},{8,10},{12,14},{16,18},{20,22},{24,26},{28,30},{2,0},{... | collective-permute-start | bytes 49160 | tf_op jit(solution)/shard_map/ppermute | solution.py:463
  17.6 5.9 %collective-permute-start.4 = (f32[16,256]{1,0:T(8,128)S(1)}, f32[16,256]{1,0:T(8,128)S(1)}, u32[]{:S(2)}, u32[]{:S(2)}) collective-permute-start(f32[16,256]{1,0:T(8,128)S(1)} %get-tuple-element.75), channel_id=1, source_target_pairs={{2,4},{6,8},{10,12},{14,16},{18,20},{22,24},{26,28},{30,0},{4,2},{... | collective-permute-start | bytes 49160 | tf_op jit(solution)/shard_map/ppermute | solution.py:462
  19.8 3.7 %collective-permute-start.5 = (f32[16,256]{1,0:T(8,128)S(1)}, f32[16,256]{1,0:T(8,128)S(1)}, u32[]{:S(2)}, u32[]{:S(2)}) collective-permute-start(f32[16,256]{1,0:T(8,128)S(1)} %get-tuple-element.76), channel_id=1, source_target_pairs={{0,1},{1,0},{2,3},{3,2},{4,5},{5,4},{6,7},{7,6},{8,9},{9,8},{10,11... | collective-permute-start | bytes 49160 | tf_op jit(solution)/shard_map/ppermute | solution.py:465

commit v4 on v3

--- a/solution.py
+++ b/solution.py
@@ -70,18 +70,13 @@
     return jnp.concatenate([high.astype(F32), low.astype(F32)], axis=0).astype(BF16)
 
 
-def spread(columns):
+def turns(columns):
     first, even = halves(8)
     tiles = []
     for column in columns[:2]:
-        turned = roll(column, 64)
-        for pair in (jnp.where(first, column, turned), jnp.where(first, turned, column)):
-            moved = roll(pair, 32)
-            tiles.append(jnp.where(even, pair, moved))
-            tiles.append(jnp.where(even, moved, pair))
+        tiles += [column] + [roll(column, 128 - 32 * s) for s in range(1, 4)]
     pair = jnp.where(first, columns[2], roll(columns[2], 64))
-    tiles.append(jnp.where(even, pair, roll(pair, 32)))
-    return tiles
+    return tiles + [jnp.where(even, pair, roll(pair, 32))]
 
 
 def group_swap(parts):
@@ -97,12 +92,16 @@
 
 
 def place_rows(source, target, start, members):
+    def piece(q, d, group):
+        order = [4 * c + (group + s) % 4 for c in range(2) for s in range(4)] + [Q - 1]
+        return jnp.concatenate([source[q, p : p + 1, d, :] for p in order], axis=0)
+
     for d in members:
         for c in range(2):
             target[start + d * 16 : start + d * 16 + Q, c * 128 : c * 128 + 128] = group_place(
-                [source[q, :, d, :] for q in range(4 * c, 4 * c + 4)]
+                [piece(4 * c + g, d, g) for g in range(4)]
             )
-    target[start : start + Q, 256:W] = group_place([source[Q - 1, :, d, :] for d in members])
+    target[start : start + Q, 256:W] = group_place([piece(Q - 1, d, g) for g, d in enumerate(members)])
 
 
 def group_place(parts):
@@ -113,7 +112,7 @@
 
 def weigh(rows_of, x_ref, y_ref, count):
     for tile in range(M // 8):
-        spans = spread([x_ref[tile * 8 : tile * 8 + 8, c * 128 : c * 128 + 128] for c in range(3)])
+        spans = turns([x_ref[tile * 8 : tile * 8 + 8, c * 128 : c * 128 + 128] for c in range(3)])
 
         def mixed(row, column):
             total = rows_of[row : row + 1, column : column + 128] * spans[0]
@@ -122,15 +121,22 @@
             return total
 
         for d in range(count):
-            start = d * M + tile * 8
+            start = (tile * count + d) * 8
             for c in range(2):
                 y_ref[start : start + 8, c * 128 : c * 128 + 128] = mixed(d * 16, c * 128)
         for pack in range(0, count, 4):
             total = mixed(pack * 16, 256)
             for d in range(pack, min(pack + 4, count)):
-                start = d * M + tile * 8
+                start = (tile * count + d) * 8
                 moved = roll(total, 128 - 32 * (d - pack)) if d > pack else total
                 y_ref[start : start + 8, 256:W] = moved
+
+
+def order_rows(tall, matrices):
+    for d, matrix in enumerate(matrices):
+        for tile in range(M // 8):
+            start = (tile * len(matrices) + d) * 8
+            tall[start : start + 8, 0:M] = matrix[tile * 8 : tile * 8 + 8]
 
 
 def predict(star, left, x_ref, y_ref, first_ref, second_ref):
@@ -165,7 +171,7 @@
 
 def send_rows(pick, tab_ref):
     high, low = split(tab_ref[...])
-    return dot_nt(pick, high) + dot_nt(pick, low)
+    return dot_nt(jnp.concatenate([pick, pick], axis=1), jnp.concatenate([high, low], axis=1))
 
 
 def off_rank():
@@ -210,16 +216,14 @@
     star_out[...] = jnp.zeros((48, W), F32)
     place_rows(star_in, star_out, 0, range(3))
     tall[...] = jnp.zeros((W, LANES), F32)
-    for d in range(3):
-        tall[d * M : d * M + M, 0:M] = stiff_in[d]
+    order_rows(tall, [stiff_in[d] for d in range(3)])
     left_out[...] = stack_split(tall[0:256, :].T[0:M, 0 : 3 * M + 8])
     tall[0 : 4 * JP, :] = jnp.zeros((4 * JP, LANES), F32)
     for f in range(4):
         tall[f * JP : f * JP + J, 0:M] = proj_in[:, f, :]
-    values = tall[0 : 4 * JP, :].T[0:M]
+    values = tall[0 : 4 * JP, 0:M]
     high = values.astype(BF16).astype(F32)
-    stacked = jnp.concatenate([high, values - high, high, jnp.zeros((LANES * 2 - 3 * M, 4 * JP), F32)], axis=0)
-    proj_out[...] = stacked.T[:, 0 : 3 * M].astype(BF16)
+    proj_out[...] = jnp.concatenate([high, values - high, high], axis=1).astype(BF16)
     slots = elem_in.shape[2]
     slot_pad[0:1, 0:slots] = face_in[0] * E + elem_in[0] + 1
     rows = 32 + 16 * n_off
@@ -240,7 +244,7 @@
 
 def gather_local(pick, tab_ref):
     high, low = split(tab_ref[0 : Q * JP + 8, :])
-    return dot(high, pick) + dot(low, pick)
+    return dot(jnp.concatenate([high, low], axis=1), jnp.concatenate([pick, pick], axis=0))
 
 
 def side_kernel(
@@ -281,10 +285,7 @@
     for q in range(Q):
         fnbr_out[q * 16 : q * 16 + Q, :] = group_place([nbr_in[q, :, f, :] for f in range(4)])
     tall[...] = jnp.zeros((512, LANES), F32)
-    for f in range(4):
-        tall[f * M : f * M + M, 0:M] = minus_in[f]
-    for d in range(3):
-        tall[(4 + d) * M : (5 + d) * M, 0:M] = vol_in[d]
+    order_rows(tall, [minus_in[f] for f in range(4)] + [vol_in[d] for d in range(3)])
     left_out[...] = stack_split(tall[...].T[0:M, 0 : 7 * M + 8])
     turn_pad[...] = jnp.zeros((3 * JP, LANES), F32)
     for o in range(3):
@@ -293,13 +294,17 @@
     lift_pad[...] = jnp.zeros((LANES, LANES), F32)
     for f in range(4):
         lift_pad[0:J, 0:M] = lift_in[:, f, :]
-        tall[f * 3 * JP : (f + 1) * 3 * JP, :] = lax.dot_general(
+        combined = lax.dot_general(
             turn_pad[...],
             lift_pad[...],
             (((1,), (0,)), ((), ())),
             precision=lax.Precision.HIGHEST,
             preferred_element_type=F32,
         )
+        for o in range(3):
+            for tile in range(3):
+                start = (tile * 12 + f * 3 + o) * 8
+                tall[start : start + 8, :] = combined[o * JP + tile * 8 : o * JP + tile * 8 + 8]
     lift_out[...] = stack_split(tall[...].T[0:M, 0 : 12 * JP])
     ipad[...] = jnp.zeros((8, LANES), jnp.int32)
     index_row = group_place([index_in[f : f + 1, :] for f in range(4)])
@@ -317,7 +322,8 @@
     place = jnp.where(
         row < 32, LANES + (row ^ turned_around()), jnp.where(within < SO, LANES + 32 + source * SO + within, -1)
     )
-    pick_far_out[...] = jnp.where(place == index_row, 1.0, 0.0).astype(BF16)
+    pick_far = jnp.where(place == index_row, 1.0, 0.0)
+    pick_far_out[...] = jnp.concatenate([pick_far, pick_far], axis=0).astype(BF16)
     here_out[...] = gather_local(pick_here, tab)
     tall[...] = jnp.zeros((512, LANES), F32)
     for q in range(Q):
@@ -351,9 +357,10 @@
     stage[32:48, :] = own[...]
     for k, ref in enumerate(offs):
         stage[48 + 16 * k : 64 + 16 * k, :] = ref[...]
-    turned = stage[...].T[0 : Q * JP + 8, :]
-    high, low = split(turned)
-    return dot(high, pick_far[...]) + dot(low, pick_far[...])
+    rows = stage[...]
+    high = rows.astype(BF16).astype(F32)
+    turned = jnp.concatenate([high, rows - high], axis=0).T[0 : Q * JP + 8, :].astype(BF16)
+    return dot(turned, pick_far[...])
 
 
 def neighbour_flux(near_ref, fnbr, flags, lift, y_ref):
@@ -372,7 +379,7 @@
             for f in range(4):
                 facing = flags[f : f + 1, :]
                 for o in range(3):
-                    start = (f * 3 + o) * JP + tile * 8
+                    start = (tile * 12 + f * 3 + o) * 8
                     y_ref[start : start + 8, c * 128 : c * 128 + 128] = jnp.where(
                         facing == o, swapped[f], 0.0
                     )
@@ -560,7 +567,7 @@
             shape(2 * M, 12 * JP, dtype=BF16),
             near,
             shape(LANES, LANES, dtype=BF16),
-            shape(rows, LANES, dtype=BF16),
+            shape(2 * rows, LANES, dtype=BF16),
             shape(8, LANES, dtype=jnp.int32),
             wide,
         ],

time: 25.1 us -> 24.7 us (0.984)
  Pallas kernels: 10.7 us -> 10.2 us
    pallas_call x5, Pallas kernels: 10.7 us -> 10.2 us  [call(): pl.pallas_call(kernel, in_specs=specs, out_specs=[pl.BlockSpec(memory_spa...]
where the time goes in v4:
time: 24.7 us; the launch traced here: 24.6 us
  starting transfers between devices  11.5 us (47%)
  Pallas kernels  10.2 us (41%)
  waiting for transfers between devices  2.69 us (11%)
    pallas_call x5, Pallas kernels, call(): pl.pallas_call(kernel, in_specs=specs, out_specs=[pl.BlockSpec(memory_spa...  10.2 us
    ppermute x2, starting transfers between devices, trade(): got_far = lax.ppermute(far, 'fault', exchange(1))  7.84 us
    ppermute x2, starting transfers between devices, trade(): lax.ppermute(rows, 'off', [(j, (j + k) % n_off) for j in range(n_off)])  2.99 us
    ppermute x2, waiting for transfers between devices, trade(): got_far = lax.ppermute(far, 'fault', exchange(1))  1.54 us
    ppermute x2, waiting for transfers between devices, trade(): lax.ppermute(rows, 'off', [(j, (j + k) % n_off) for j in range(n_off)])  1.15 us
    ppermute x2, starting transfers between devices, trade(): got_chip = lax.ppermute(chip, 'fault', exchange(0))  0.67 us
  transfers between devices with their start and end apart: 6, of which 2 were waited for; matrix products, arithmetic and copies ran while one was open for 0% of the time, Pallas kernels for 7%

profile of v4, /device:TPU:0, one launch (start us, length us, event | category | flops | bytes accessed | tf_op | source)
XLA Modules:
  0.0 24.6 jit_solution(12462607085741174885)
XLA Ops:
  0.0 0.0 copy-start
  0.0 0.0 copy-start.1
  0.0 0.0 copy-start.2
  0.0 0.0 copy-start.3
  0.0 0.0 copy-start.4
  0.0 0.0 copy-start.5
  0.0 0.0 copy-start.6
  0.0 3.9 %shard_map.163 = (s32[4,32]{1,0:T(4,128)S(1)}, s32[4,32]{1,0:T(4,128)S(1)}, s32[1,32]{1,0:T(1,128)S(1)}, s32[1,16]{1,0:T(1,128)S(1)}, f32[56,384]{1,0:T(8,128)S(...) custom-call(f32[9,32,56]{2,1,0:T(8,128)} %bitcast.15, ...), custom_call_target="tpu_custom_call" | custom-call | flops 2000000000 | bytes 2000000 | tf_op jit(solution)/shard_map/pallas_call | solution.py:451
  4.0 0.6 %collective-permute-start = (f32[16,256]{1,0:T(8,128)S(1)}, f32[16,256]{1,0:T(8,128)S(1)}, u32[]{:S(2)}, u32[]{:S(2)}) collective-permute-start(f32[16,256]{1,0:T(8,128)S(1)} %get-tuple-element.60), channel_id=1, source_target_pairs={{0,2},{4,6},{8,10},{12,14},{16,18},{20,22},{24,26},{28,30},{2,0},{... | collective-permute-start | bytes 49160 | tf_op jit(solution)/shard_map/ppermute | solution.py:470
  4.6 5.7 %collective-permute-start.1 = (f32[16,256]{1,0:T(8,128)S(1)}, f32[16,256]{1,0:T(8,128)S(1)}, u32[]{:S(2)}, u32[]{:S(2)}) collective-permute-start(f32[16,256]{1,0:T(8,128)S(1)} %get-tuple-element.61), channel_id=1, source_target_pairs={{2,4},{6,8},{10,12},{14,16},{18,20},{22,24},{26,28},{30,0},{4,2},{... | collective-permute-start | bytes 49160 | tf_op jit(solution)/shard_map/ppermute | solution.py:469
  10.2 1.5 %collective-permute-start.2 = (f32[16,256]{1,0:T(8,128)S(1)}, f32[16,256]{1,0:T(8,128)S(1)}, u32[]{:S(2)}, u32[]{:S(2)}) collective-permute-start(f32[16,256]{1,0:T(8,128)S(1)} %get-tuple-element.62), channel_id=1, source_target_pairs={{0,1},{1,0},{2,3},{3,2},{4,5},{5,4},{6,7},{7,6},{8,9},{9,8},{10,11... | collective-permute-start | bytes 49160 | tf_op jit(solution)/shard_map/ppermute | solution.py:472
  11.7 0.0 copy-done
  11.7 0.0 copy-done.1
  11.7 0.0 copy-done.2
  11.7 0.0 copy-done.3
  11.7 0.0 copy-done.4
  11.7 0.0 copy-done.5
  11.7 0.0 copy-done.6
  11.7 1.0 %shard_map.164 = (f32[56,384]{1,0:T(8,128)S(1)}, f32[112,384]{1,0:T(8,128)S(1)}, f32[144,128]{1,0:T(8,128)S(1)}, bf16[112,400]{1,0:T(8,128)(2,1)S(1)}, bf16[112,...) custom-call(f32[56,384]{1,0:T(8,128)S(1)} %get-tuple-element.41.firs, ...), custom_call_target="tpu_custom_call" | custom-call | flops 2000000000 | bytes 2000000 | tf_op jit(solution)/shard_map/pallas_call | solution.py:451
  12.8 0.0 collective-permute-done.chip
  12.8 0.0 collective-permute-done.1.far
  12.8 1.1 %collective-permute-done.2.refs_0_ = f32[16,256]{1,0:T(8,128)S(1)} collective-permute-done((f32[16,256]{1,0:T(8,128)S(1)}, f32[16,256]{1,0:T(8,128)S(1)}, u32[]{:S(2)}, u32[]{:S(2)}) %collective-permute-start.2) | collective-permute-done | bytes 16416 | tf_op jit(solution)/shard_map/ppermute | solution.py:472
  14.0 3.2 %shard_map.165 = (f32[224,128]{1,0:T(8,128)S(1)}, f32[56,384]{1,0:T(8,128)S(1)}, f32[56,384]{1,0:T(8,128)S(1)}, f32[256,128]{1,0:T(8,128)S(1)}, f32[16,256]{1,0:...) custom-call(f32[56,384]{1,0:T(8,128)S(1)} %get-tuple-element.43.state, ...), custom_call_target="tpu_custom_call" | custom-call | flops 2000000000 | bytes 2000000 | tf_op jit(solution)/shard_map/pallas_call | solution.py:451
  17.1 0.1 collective-permute-start.3
  17.2 2.2 %collective-permute-start.4 = (f32[16,256]{1,0:T(8,128)S(1)}, f32[16,256]{1,0:T(8,128)S(1)}, u32[]{:S(2)}, u32[]{:S(2)}) collective-permute-start(f32[16,256]{1,0:T(8,128)S(1)} %get-tuple-element.75), channel_id=1, source_target_pairs={{2,4},{6,8},{10,12},{14,16},{18,20},{22,24},{26,28},{30,0},{4,2},{... | collective-permute-start | bytes 49160 | tf_op jit(solution)/shard_map/ppermute | solution.py:469
  19.4 1.5 %collective-permute-start.5 = (f32[16,256]{1,0:T(8,128)S(1)}, f32[16,256]{1,0:T(8,128)S(1)}, u32[]{:S(2)}, u32[]{:S(2)}) collective-permute-start(f32[16,256]{1,0:T(8,128)S(1)} %get-tuple-element.76), channel_id=1, source_target_pairs={{0,1},{1,0},{2,3},{3,2},{4,5},{5,4},{6,7},{7,6},{8,9},{9,8},{10,11... | collective-permute-start | bytes 49160 | tf_op jit(solution)/shard_map/ppermute | solution.py:472
  20.9 0.7 %shard_map.166 = (f32[56,384]{1,0:T(8,128)S(1)}, f32[224,128]{1,0:T(8,128)S(1)}) custom-call(f32[56,384]{1,0:T(8,128)S(1)} %get-tuple-element.41.first_in.first, f32[56,384]{1,0:T(8,128)S(1)} %get-tuple-element.42.second, f32[56,384]{1,0:T(8,128)S(1)} %get-tuple-element.63.later, f32[56,384]{1,0:T(8,128)S(1)} %get-tuple-element.64.half, ...), custom_call_target="tpu_custom_call" | custom-call | flops 2000000000 | bytes 2000000 | tf_op jit(solution)/shard_map/pallas_call | solution.py:451
  21.6 0.0 collective-permute-done.3.chip
  21.6 1.5 %collective-permute-done.4.far = f32[16,256]{1,0:T(8,128)S(1)} collective-permute-done((f32[16,256]{1,0:T(8,128)S(1)}, f32[16,256]{1,0:T(8,128)S(1)}, u32[]{:S(2)}, u32[]{:S(2)}) %collective-permute-start.4) | collective-permute-done | bytes 16416 | tf_op jit(solution)/shard_map/ppermute | solution.py:469
  23.1 0.0 collective-permute-done.5.refs_0_
  23.1 1.4 %shard_map.167 = f32[9,32,56]{2,1,0:T(8,128)} custom-call(f32[56,384]{1,0:T(8,128)S(1)} %get-tuple-element.71.base, f32[224,128]{1,0:T(8,128)S(1)} %get-tuple-element.72.here, f32[144,128]{1,0:T(8,128)S(1)} %get-tuple-element.52.fnbr, s32[8,128]{1,0:T(8,128)S(1)} %get-tuple-element.53.flags, bf16[112,288]{1,0:T(8,128)(2,1)S(1)} %get-tuple-element.54.lift, ...), custom_call_target="tpu_custom_call" | custom-call | flops 2000000000 | bytes 2000000 | tf_op jit(solution)/shard_map/pallas_call | solution.py:451
Async XLA Ops:
  0.0 11.7 %copy-start = (f32[4,9,9,32]{3,0,2,1:T(4,128)S(1)}, f32[4,9,9,32]{3,0,2,1:T(4,128)}, u32[]{:S(2)}) copy-start(f32[4,9,9,32]{3,0,2,1:T(4,128)} %param.19) | copy-start | bytes 124420
  0.0 11.7 %copy-start.1 = (f32[4,9,9,32]{3,0,2,1:T(4,128)S(1)}, f32[4,9,9,32]{3,0,2,1:T(4,128)}, u32[]{:S(2)}) copy-start(f32[4,9,9,32]{3,0,2,1:T(4,128)} %param.20) | copy-start | bytes 124420
  0.0 11.7 %copy-start.2 = (f32[4,56,56]{2,1,0:T(8,128)S(1)}, f32[4,56,56]{2,1,0:T(8,128)}, u32[]{:S(2)}) copy-start(f32[4,56,56]{2,1,0:T(8,128)} %minus_in.1) | copy-start | bytes 150532
  0.0 11.7 %copy-start.3 = (f32[3,56,56]{2,1,0:T(8,128)S(1)}, f32[3,56,56]{2,1,0:T(8,128)}, u32[]{:S(2)}) copy-start(f32[3,56,56]{2,1,0:T(8,128)} %vol_in.1) | copy-start | bytes 112900
  0.0 11.7 %copy-start.4 = (f32[16,9,56]{2,0,1:T(8,128)S(1)}, f32[16,9,56]{2,0,1:T(8,128)}, u32[]{:S(2)}) copy-start(f32[16,9,56]{2,0,1:T(8,128)} %param.33) | copy-start | bytes 96772
  0.0 11.7 %copy-start.5 = (f32[4,21,56]{2,0,1:T(4,128)S(1)}, f32[4,21,56]{2,0,1:T(4,128)}, u32[]{:S(2)}) copy-start(f32[4,21,56]{2,0,1:T(4,128)} %param.26) | copy-start | bytes 56452
  0.0 11.7 %copy-start.6 = (f32[3,21,21]{2,1,0:T(8,128)S(1)}, f32[3,21,21]{2,1,0:T(8,128)}, u32[]{:S(2)}) copy-start(f32[3,21,21]{2,1,0:T(8,128)} %turn_in.1) | copy-start | bytes 15880
  4.0 8.8 %collective-permute-start = (f32[16,256]{1,0:T(8,128)S(1)}, f32[16,256]{1,0:T(8,128)S(1)}, u32[]{:S(2)}, u32[]{:S(2)}) collective-permute-start(f32[16,256]{1,0:T(8,128)S(1)} %get-tuple-element.60), channel_id=1, source_target_pairs={{0,2},{4,6},{8,10},{12,14},{16,18},{20,22},{24,26},{28,30},{2,0},{... | collective-permute-start | bytes 49160 | tf_op jit(solution)/shard_map/ppermute | solution.py:470
  4.6 8.2 %collective-permute-start.1 = (f32[16,256]{1,0:T(8,128)S(1)}, f32[16,256]{1,0:T(8,128)S(1)}, u32[]{:S(2)}, u32[]{:S(2)}) collective-permute-start(f32[16,256]{1,0:T(8,128)S(1)} %get-tuple-element.61), channel_id=1, source_target_pairs={{2,4},{6,8},{10,12},{14,16},{18,20},{22,24},{26,28},{30,0},{4,2},{... | collective-permute-start | bytes 49160 | tf_op jit(solution)/shard_map/ppermute | solution.py:469
  10.2 3.7 %collective-permute-start.2 = (f32[16,256]{1,0:T(8,128)S(1)}, f32[16,256]{1,0:T(8,128)S(1)}, u32[]{:S(2)}, u32[]{:S(2)}) collective-permute-start(f32[16,256]{1,0:T(8,128)S(1)} %get-tuple-element.62), channel_id=1, source_target_pairs={{0,1},{1,0},{2,3},{3,2},{4,5},{5,4},{6,7},{7,6},{8,9},{9,8},{10,11... | collective-permute-start | bytes 49160 | tf_op jit(solution)/shard_map/ppermute | solution.py:472
  17.1 4.5 %collective-permute-start.3 = (f32[16,256]{1,0:T(8,128)S(1)}, f32[16,256]{1,0:T(8,128)S(1)}, u32[]{:S(2)}, u32[]{:S(2)}) collective-permute-start(f32[16,256]{1,0:T(8,128)S(1)} %get-tuple-element.74), channel_id=1, source_target_pairs={{0,2},{4,6},{8,10},{12,14},{16,18},{20,22},{24,26},{28,30},{2,0},{... | collective-permute-start | bytes 49160 | tf_op jit(solution)/shard_map/ppermute | solution.py:470
  17.2 5.9 %collective-permute-start.4 = (f32[16,256]{1,0:T(8,128)S(1)}, f32[16,256]{1,0:T(8,128)S(1)}, u32[]{:S(2)}, u32[]{:S(2)}) collective-permute-start(f32[16,256]{1,0:T(8,128)S(1)} %get-tuple-element.75), channel_id=1, source_target_pairs={{2,4},{6,8},{10,12},{14,16},{18,20},{22,24},{26,28},{30,0},{4,2},{... | collective-permute-start | bytes 49160 | tf_op jit(solution)/shard_map/ppermute | solution.py:469
  19.4 3.7 %collective-permute-start.5 = (f32[16,256]{1,0:T(8,128)S(1)}, f32[16,256]{1,0:T(8,128)S(1)}, u32[]{:S(2)}, u32[]{:S(2)}) collective-permute-start(f32[16,256]{1,0:T(8,128)S(1)} %get-tuple-element.76), channel_id=1, source_target_pairs={{0,1},{1,0},{2,3},{3,2},{4,5},{5,4},{6,7},{7,6},{8,9},{9,8},{10,11... | collective-permute-start | bytes 49160 | tf_op jit(solution)/shard_map/ppermute | solution.py:472

commit v5 on v4

--- a/solution.py
+++ b/solution.py
@@ -116,7 +116,7 @@
 
         def mixed(row, column):
             total = rows_of[row : row + 1, column : column + 128] * spans[0]
-            for p in range(1, Q):
+            for p in (4, 1, 5, 2, 6, 3, 7, 8):
                 total = total + rows_of[row + p : row + p + 1, column : column + 128] * spans[p]
             return total
 
@@ -210,14 +210,14 @@
         copy.wait()
     for q in range(Q):
         tall[q * E : q * E + E, 0:M] = state_in[q]
-    state = tall[...].T[0:M, :]
-    x_ref[...] = state
-    state_out[...] = state
+    x_ref[:, Q * E : W] = jnp.zeros((M, W - Q * E), F32)
+    x_ref[:, 0 : Q * E] = tall[0 : Q * E, :].T[0:M]
+    state_out[...] = x_ref[...]
     star_out[...] = jnp.zeros((48, W), F32)
     place_rows(star_in, star_out, 0, range(3))
     tall[...] = jnp.zeros((W, LANES), F32)
     order_rows(tall, [stiff_in[d] for d in range(3)])
-    left_out[...] = stack_split(tall[0:256, :].T[0:M, 0 : 3 * M + 8])
+    left_out[...] = stack_split(tall[0 : 3 * M + 8, :].T[0:M])
     tall[0 : 4 * JP, :] = jnp.zeros((4 * JP, LANES), F32)
     for f in range(4):
         tall[f * JP : f * JP + J, 0:M] = proj_in[:, f, :]
@@ -351,12 +351,12 @@
     part_out[...] = product(left_out[...], y_ref[...])
 
 
-def arrive(chip, far, own, offs, pick_far, stage):
-    stage[0:16, :] = chip[...]
+def arrive(n_off, chip, far, own, offs, pick_far, stage):
+    stage[0:16, :] = chip[0][...] + chip[1][...]
     stage[16:32, :] = far[...]
     stage[32:48, :] = own[...]
-    for k, ref in enumerate(offs):
-        stage[48 + 16 * k : 64 + 16 * k, :] = ref[...]
+    for k in range(n_off - 1):
+        stage[48 + 16 * k : 64 + 16 * k, :] = offs[2 * k][...] + offs[2 * k + 1][...]
     rows = stage[...]
     high = rows.astype(BF16).astype(F32)
     turned = jnp.concatenate([high, rows - high], axis=0).T[0 : Q * JP + 8, :].astype(BF16)
@@ -392,14 +392,15 @@
 
 
 def middle_kernel(
-    n_off, state, second, part, here, fnbr, flags, lift, star, left, proj, pick, pick_far, own, chip, far, *refs
+    n_off, state, second, part, here, fnbr, flags, lift, star, left, proj, pick, pick_far, own, lead, rest, far, *refs
 ):
-    offs = refs[: n_off - 1]
-    outs = refs[n_off - 1 :]
+    chip = (lead, rest)
+    offs = refs[: 2 * (n_off - 1)]
+    outs = refs[2 * (n_off - 1) :]
     near_out, half_out, later_out, tab_out, far_out, chip_out, own_out = outs[:7]
     off_outs = outs[7 : 7 + n_off - 1]
     x_ref, y_ref, stage, acc = outs[7 + n_off - 1 :]
-    near_out[...] = here[...] + arrive(chip, far, own, offs, pick_far, stage)
+    near_out[...] = here[...] + arrive(n_off, chip, far, own, offs, pick_far, stage)
     total = part[...] + neighbour_flux(near_out, fnbr, flags, lift, y_ref)
     fine = jnp.concatenate([wide_fine(flags)] * 3, axis=1)
     base = state[...]
@@ -425,11 +426,12 @@
     here_out[...] = gather_local(pick_here[...], tab) + jnp.where(row, 0.0, near_first[...])
 
 
-def last_kernel(n_off, base, here, fnbr, flags, lift, pick_far, own, chip, far, *refs):
-    offs = refs[: n_off - 1]
-    out, near, y_ref, stage, tall = refs[n_off - 1 :]
+def last_kernel(n_off, base, here, fnbr, flags, lift, pick_far, own, lead, rest, far, *refs):
+    chip = (lead, rest)
+    offs = refs[: 2 * (n_off - 1)]
+    out, near, y_ref, stage, tall = refs[2 * (n_off - 1) :]
     tall[M:LANES, :] = jnp.zeros((LANES - M, W), F32)
-    near[...] = here[...] + arrive(chip, far, own, offs, pick_far, stage)
+    near[...] = here[...] + arrive(n_off, chip, far, own, offs, pick_far, stage)
     total = base[...] + neighbour_flux(near, fnbr, flags, lift, y_ref)
     tall[0:M, :] = total
     turned = tall[...].T
@@ -460,17 +462,24 @@
 
 
 def trade(far, chip, offs, n_fault, n_off):
-    def exchange(offset):
-        firsts = range(offset, n_fault, 2)
+    both = ("fault", "off")
+
+    def chip_pairs(firsts):
         pairs = [(i, (i + 1) % n_fault) for i in firsts]
-        return pairs + [(j, i) for i, j in pairs]
-
-    got = []
-    got_far = lax.ppermute(far, "fault", exchange(1))
-    got_chip = lax.ppermute(chip, "fault", exchange(0))
-    for k, rows in enumerate(offs, 1):
-        got.append(lax.ppermute(rows, "off", [(j, (j + k) % n_off) for j in range(n_off)]))
-    return got_chip, got_far, got
+        return [(a * n_off + j, b * n_off + j) for i, k in pairs for a, b in ((i, k), (k, i)) for j in range(n_off)]
+
+    def off_pairs(ranks, step):
+        return [(i * n_off + j, i * n_off + (j + step) % n_off) for i in ranks for j in range(n_off)]
+
+    chips, offs_got = [], [[] for _ in offs]
+    chips.append(lax.ppermute(chip, both, chip_pairs([0])))
+    for k, rows in enumerate(offs):
+        offs_got[k].append(lax.ppermute(rows, both, off_pairs([0], k + 1)))
+    got_far = lax.ppermute(far, both, chip_pairs(range(1, n_fault, 2)))
+    chips.append(lax.ppermute(chip, both, chip_pairs(range(2, n_fault, 2))))
+    for k, rows in enumerate(offs):
+        offs_got[k].append(lax.ppermute(rows, both, off_pairs(range(1, n_fault), k + 1)))
+    return chips, got_far, sum(offs_got, [])
 
 
 def on_device(
@@ -581,7 +590,7 @@
     )
     outs = call(
         functools.partial(middle_kernel, n_off),
-        (state, second, part, here, fnbr, flags, lift, star, left, proj, pick, pick_far, own, got_chip, got_far, *got_off),
+        (state, second, part, here, fnbr, flags, lift, star, left, proj, pick, pick_far, own, *got_chip, got_far, *got_off),
         [near, wide, wide, table] + [block] * (3 + n_off - 1),
         [vmem((M, W), F32), vmem((12 * JP, W), F32), vmem((rows, TAB), F32), vmem((M, W), F32)],
     )
@@ -595,7 +604,7 @@
     )
     (result,) = call(
         functools.partial(last_kernel, n_off),
-        (base, here, fnbr, flags, lift, pick_far, own, got_chip, got_far, *got_off),
+        (base, here, fnbr, flags, lift, pick_far, own, *got_chip, got_far, *got_off),
         [shape(Q, E, M)],
         [vmem((Q * JP + 8, LANES), F32), vmem((12 * JP, W), F32), vmem((rows, TAB), F32), vmem((LANES, W), F32)],
     )

time: 24.7 us -> 34.6 us (1.40)
  starting transfers between devices: 11.5 us -> 22.4 us
  waiting for transfers between devices: 2.69 us -> 1.47 us
    ppermute x6 -> x10, starting transfers between devices: 11.5 us -> 22.4 us  [the longest x2 8.65 us: trade(): got_far = lax.ppermute(far, both, chip_pairs(range(1, n_fault, 2)))]
    ppermute x6 -> x10, waiting for transfers between devices: 2.69 us -> 1.47 us  [the longest x2 1.45 us: trade(): got_far = lax.ppermute(far, both, chip_pairs(range(1, n_fault, 2)))]
  transfers between devices with their start and end apart: 6 -> 10, of which waited for: 2 -> 2; matrix products, arithmetic and copies ran while one was open for 0% -> 0% of each run, Pallas kernels for 7% -> 5%
where the time goes in v5:
time: 34.6 us; the launch traced here: 34.4 us
  starting transfers between devices  22.4 us (65%)
  Pallas kernels  10.3 us (30%)
  waiting for transfers between devices  1.47 us (4%)
    pallas_call x5, Pallas kernels, call(): pl.pallas_call(kernel, in_specs=specs, out_specs=[pl.BlockSpec(memory_spa...  10.3 us
    ppermute x2, starting transfers between devices, trade(): got_far = lax.ppermute(far, both, chip_pairs(range(1, n_fault, 2)))  8.65 us
    ppermute x2, starting transfers between devices, trade(): offs_got[k].append(lax.ppermute(rows, both, off_pairs([0], k + 1)))  6.8 us
    ppermute x2, starting transfers between devices, trade(): chips.append(lax.ppermute(chip, both, chip_pairs([0])))  4.36 us
    ppermute x2, waiting for transfers between devices, trade(): got_far = lax.ppermute(far, both, chip_pairs(range(1, n_fault, 2)))  1.45 us
    ppermute x2, starting transfers between devices, trade(): chips.append(lax.ppermute(chip, both, chip_pairs(range(2, n_fault, 2))))  1.32 us
    ppermute x2, starting transfers between devices, trade(): lax.ppermute(rows, both, off_pairs(range(1, n_fault), k + 1))  1.32 us
  transfers between devices with their start and end apart: 10, of which 2 were waited for; matrix products, arithmetic and copies ran while one was open for 0% of the time, Pallas kernels for 5%

profile of v5, /device:TPU:0, one launch (start us, length us, event | category | flops | bytes accessed | tf_op | source)
XLA Modules:
  0.0 34.4 jit_solution(17604408423304535748)
XLA Ops:
  0.0 0.0 copy-start
  0.0 0.0 copy-start.1
  0.0 0.0 copy-start.2
  0.0 0.0 copy-start.3
  0.0 0.0 copy-start.4
  0.0 0.0 copy-start.5
  0.0 0.0 copy-start.6
  0.0 3.9 %shard_map.163 = (s32[4,32]{1,0:T(4,128)S(1)}, s32[4,32]{1,0:T(4,128)S(1)}, s32[1,32]{1,0:T(1,128)S(1)}, s32[1,16]{1,0:T(1,128)S(1)}, f32[56,384]{1,0:T(8,128)S(...) custom-call(f32[9,32,56]{2,1,0:T(8,128)} %bitcast.15, ...), custom_call_target="tpu_custom_call" | custom-call | flops 2000000000 | bytes 2000000 | tf_op jit(solution)/shard_map/pallas_call | solution.py:453
  4.0 0.7 %collective-permute-start.1 = (f32[16,256]{1,0:T(8,128)S(1)}, f32[16,256]{1,0:T(8,128)S(1)}, u32[]{:S(2)}, u32[]{:S(2)}) collective-permute-start(f32[16,256]{1,0:T(8,128)S(1)} %get-tuple-element.60), channel_id=1, source_target_pairs={{4,6},{5,7},{6,4},{7,5},{8,10},{9,11},{10,8},{11,9},{12,14},{13,15... | collective-permute-start | bytes 49160 | tf_op jit(solution)/shard_map/ppermute | solution.py:479
  4.6 2.4 %collective-permute-start = (f32[16,256]{1,0:T(8,128)S(1)}, f32[16,256]{1,0:T(8,128)S(1)}, u32[]{:S(2)}, u32[]{:S(2)}) collective-permute-start(f32[16,256]{1,0:T(8,128)S(1)} %get-tuple-element.60), channel_id=1, source_target_pairs={{0,2},{1,3},{2,0},{3,1}} | collective-permute-start | bytes 49160 | tf_op jit(solution)/shard_map/ppermute | solution.py:475
  7.1 0.7 %collective-permute-start.4 = (f32[16,256]{1,0:T(8,128)S(1)}, f32[16,256]{1,0:T(8,128)S(1)}, u32[]{:S(2)}, u32[]{:S(2)}) collective-permute-start(f32[16,256]{1,0:T(8,128)S(1)} %get-tuple-element.62), channel_id=1, source_target_pairs={{2,3},{3,2},{4,5},{5,4},{6,7},{7,6},{8,9},{9,8},{10,11},{11,10},{1... | collective-permute-start | bytes 49160 | tf_op jit(solution)/shard_map/ppermute | solution.py:481
  7.8 4.4 %collective-permute-start.3 = (f32[16,256]{1,0:T(8,128)S(1)}, f32[16,256]{1,0:T(8,128)S(1)}, u32[]{:S(2)}, u32[]{:S(2)}) collective-permute-start(f32[16,256]{1,0:T(8,128)S(1)} %get-tuple-element.62), channel_id=1, source_target_pairs={{0,1},{1,0}} | collective-permute-start | bytes 49160 | tf_op jit(solution)/shard_map/ppermute | solution.py:477
  12.2 4.4 %collective-permute-start.2 = (f32[16,256]{1,0:T(8,128)S(1)}, f32[16,256]{1,0:T(8,128)S(1)}, u32[]{:S(2)}, u32[]{:S(2)}) collective-permute-start(f32[16,256]{1,0:T(8,128)S(1)} %get-tuple-element.61), channel_id=1, source_target_pairs={{2,4},{3,5},{4,2},{5,3},{6,8},{7,9},{8,6},{9,7},{10,12},{11,13},{1... | collective-permute-start | bytes 49160 | tf_op jit(solution)/shard_map/ppermute | solution.py:478
  16.6 0.0 copy-done
  16.6 0.0 copy-done.1
  16.6 0.0 copy-done.2
  16.6 0.0 copy-done.3
  16.6 0.0 copy-done.4
  16.6 0.0 copy-done.5
  16.6 0.0 copy-done.6
  16.6 1.0 %shard_map.164 = (f32[56,384]{1,0:T(8,128)S(1)}, f32[112,384]{1,0:T(8,128)S(1)}, f32[144,128]{1,0:T(8,128)S(1)}, bf16[112,400]{1,0:T(8,128)(2,1)S(1)}, bf16[112,...) custom-call(f32[56,384]{1,0:T(8,128)S(1)} %get-tuple-element.41.firs, ...), custom_call_target="tpu_custom_call" | custom-call | flops 2000000000 | bytes 2000000 | tf_op jit(solution)/shard_map/pallas_call | solution.py:453
  17.7 0.4 %collective-permute-done.2.far = f32[16,256]{1,0:T(8,128)S(1)} collective-permute-done((f32[16,256]{1,0:T(8,128)S(1)}, f32[16,256]{1,0:T(8,128)S(1)}, u32[]{:S(2)}, u32[]{:S(2)}) %collective-permute-start.2) | collective-permute-done | bytes 16416 | tf_op jit(solution)/shard_map/ppermute | solution.py:478
  18.1 0.0 collective-permute-done.1.rest
  18.1 0.0 collective-permute-done.lead
  18.1 0.0 collective-permute-done.4.refs_1_
  18.1 0.0 collective-permute-done.3.refs_0_
  18.1 3.2 %shard_map.165 = (f32[224,128]{1,0:T(8,128)S(1)}, f32[56,384]{1,0:T(8,128)S(1)}, f32[56,384]{1,0:T(8,128)S(1)}, f32[256,128]{1,0:T(8,128)S(1)}, f32[16,256]{1,0:...) custom-call(f32[56,384]{1,0:T(8,128)S(1)} %get-tuple-element.43.state, ...), custom_call_target="tpu_custom_call" | custom-call | flops 2000000000 | bytes 2000000 | tf_op jit(solution)/shard_map/pallas_call | solution.py:453
  21.3 0.7 %collective-permute-start.6 = (f32[16,256]{1,0:T(8,128)S(1)}, f32[16,256]{1,0:T(8,128)S(1)}, u32[]{:S(2)}, u32[]{:S(2)}) collective-permute-start(f32[16,256]{1,0:T(8,128)S(1)} %get-tuple-element.74), channel_id=1, source_target_pairs={{4,6},{5,7},{6,4},{7,5},{8,10},{9,11},{10,8},{11,9},{12,14},{13,15... | collective-permute-start | bytes 49160 | tf_op jit(solution)/shard_map/ppermute | solution.py:479
  22.0 1.9 %collective-permute-start.5 = (f32[16,256]{1,0:T(8,128)S(1)}, f32[16,256]{1,0:T(8,128)S(1)}, u32[]{:S(2)}, u32[]{:S(2)}) collective-permute-start(f32[16,256]{1,0:T(8,128)S(1)} %get-tuple-element.74), channel_id=1, source_target_pairs={{0,2},{1,3},{2,0},{3,1}} | collective-permute-start | bytes 49160 | tf_op jit(solution)/shard_map/ppermute | solution.py:475
  23.9 0.7 %collective-permute-start.9 = (f32[16,256]{1,0:T(8,128)S(1)}, f32[16,256]{1,0:T(8,128)S(1)}, u32[]{:S(2)}, u32[]{:S(2)}) collective-permute-start(f32[16,256]{1,0:T(8,128)S(1)} %get-tuple-element.76), channel_id=1, source_target_pairs={{2,3},{3,2},{4,5},{5,4},{6,7},{7,6},{8,9},{9,8},{10,11},{11,10},{1... | collective-permute-start | bytes 49160 | tf_op jit(solution)/shard_map/ppermute | solution.py:481
  24.6 2.4 %collective-permute-start.8 = (f32[16,256]{1,0:T(8,128)S(1)}, f32[16,256]{1,0:T(8,128)S(1)}, u32[]{:S(2)}, u32[]{:S(2)}) collective-permute-start(f32[16,256]{1,0:T(8,128)S(1)} %get-tuple-element.76), channel_id=1, source_target_pairs={{0,1},{1,0}} | collective-permute-start | bytes 49160 | tf_op jit(solution)/shard_map/ppermute | solution.py:477
  27.0 4.2 %collective-permute-start.7 = (f32[16,256]{1,0:T(8,128)S(1)}, f32[16,256]{1,0:T(8,128)S(1)}, u32[]{:S(2)}, u32[]{:S(2)}) collective-permute-start(f32[16,256]{1,0:T(8,128)S(1)} %get-tuple-element.75), channel_id=1, source_target_pairs={{2,4},{3,5},{4,2},{5,3},{6,8},{7,9},{8,6},{9,7},{10,12},{11,13},{1... | collective-permute-start | bytes 49160 | tf_op jit(solution)/shard_map/ppermute | solution.py:478
  31.2 0.7 %shard_map.166 = (f32[56,384]{1,0:T(8,128)S(1)}, f32[224,128]{1,0:T(8,128)S(1)}) custom-call(f32[56,384]{1,0:T(8,128)S(1)} %get-tuple-element.41.first_in.first, f32[56,384]{1,0:T(8,128)S(1)} %get-tuple-element.42.second, f32[56,384]{1,0:T(8,128)S(1)} %get-tuple-element.63.later, f32[56,384]{1,0:T(8,128)S(1)} %get-tuple-element.64.half, ...), custom_call_target="tpu_custom_call" | custom-call | flops 2000000000 | bytes 2000000 | tf_op jit(solution)/shard_map/pallas_call | solution.py:453
  31.9 1.0 %collective-permute-done.7.far = f32[16,256]{1,0:T(8,128)S(1)} collective-permute-done((f32[16,256]{1,0:T(8,128)S(1)}, f32[16,256]{1,0:T(8,128)S(1)}, u32[]{:S(2)}, u32[]{:S(2)}) %collective-permute-start.7) | collective-permute-done | bytes 16416 | tf_op jit(solution)/shard_map/ppermute | solution.py:478
  32.9 0.0 collective-permute-done.6.rest
  32.9 0.0 collective-permute-done.5.lead
  32.9 0.0 collective-permute-done.9.refs_1_
  32.9 0.0 collective-permute-done.8.refs_0_
  33.0 1.4 %shard_map.167 = f32[9,32,56]{2,1,0:T(8,128)} custom-call(f32[56,384]{1,0:T(8,128)S(1)} %get-tuple-element.71.base, f32[224,128]{1,0:T(8,128)S(1)} %get-tuple-element.72.here, f32[144,128]{1,0:T(8,128)S(1)} %get-tuple-element.52.fnbr, s32[8,128]{1,0:T(8,128)S(1)} %get-tuple-element.53.flags, bf16[112,288]{1,0:T(8,128)(2,1)S(1)} %get-tuple-element.54.lift, ...), custom_call_target="tpu_custom_call" | custom-call | flops 2000000000 | bytes 2000000 | tf_op jit(solution)/shard_map/pallas_call | solution.py:453
Async XLA Ops:
  0.0 16.6 %copy-start = (f32[4,9,9,32]{3,0,2,1:T(4,128)S(1)}, f32[4,9,9,32]{3,0,2,1:T(4,128)}, u32[]{:S(2)}) copy-start(f32[4,9,9,32]{3,0,2,1:T(4,128)} %param.19) | copy-start | bytes 124420
  0.0 16.6 %copy-start.1 = (f32[4,9,9,32]{3,0,2,1:T(4,128)S(1)}, f32[4,9,9,32]{3,0,2,1:T(4,128)}, u32[]{:S(2)}) copy-start(f32[4,9,9,32]{3,0,2,1:T(4,128)} %param.20) | copy-start | bytes 124420
  0.0 16.6 %copy-start.2 = (f32[4,56,56]{2,1,0:T(8,128)S(1)}, f32[4,56,56]{2,1,0:T(8,128)}, u32[]{:S(2)}) copy-start(f32[4,56,56]{2,1,0:T(8,128)} %minus_in.1) | copy-start | bytes 150532
  0.0 16.6 %copy-start.3 = (f32[3,56,56]{2,1,0:T(8,128)S(1)}, f32[3,56,56]{2,1,0:T(8,128)}, u32[]{:S(2)}) copy-start(f32[3,56,56]{2,1,0:T(8,128)} %vol_in.1) | copy-start | bytes 112900
  0.0 16.6 %copy-start.4 = (f32[16,9,56]{2,0,1:T(8,128)S(1)}, f32[16,9,56]{2,0,1:T(8,128)}, u32[]{:S(2)}) copy-start(f32[16,9,56]{2,0,1:T(8,128)} %param.33) | copy-start | bytes 96772
  0.0 16.6 %copy-start.5 = (f32[4,21,56]{2,0,1:T(4,128)S(1)}, f32[4,21,56]{2,0,1:T(4,128)}, u32[]{:S(2)}) copy-start(f32[4,21,56]{2,0,1:T(4,128)} %param.26) | copy-start | bytes 56452
  0.0 16.6 %copy-start.6 = (f32[3,21,21]{2,1,0:T(8,128)S(1)}, f32[3,21,21]{2,1,0:T(8,128)}, u32[]{:S(2)}) copy-start(f32[3,21,21]{2,1,0:T(8,128)} %turn_in.1) | copy-start | bytes 15880
  4.0 14.1 %collective-permute-start.1 = (f32[16,256]{1,0:T(8,128)S(1)}, f32[16,256]{1,0:T(8,128)S(1)}, u32[]{:S(2)}, u32[]{:S(2)}) collective-permute-start(f32[16,256]{1,0:T(8,128)S(1)} %get-tuple-element.60), channel_id=1, source_target_pairs={{4,6},{5,7},{6,4},{7,5},{8,10},{9,11},{10,8},{11,9},{12,14},{13,15... | collective-permute-start | bytes 49160 | tf_op jit(solution)/shard_map/ppermute | solution.py:479
  4.6 13.4 %collective-permute-start = (f32[16,256]{1,0:T(8,128)S(1)}, f32[16,256]{1,0:T(8,128)S(1)}, u32[]{:S(2)}, u32[]{:S(2)}) collective-permute-start(f32[16,256]{1,0:T(8,128)S(1)} %get-tuple-element.60), channel_id=1, source_target_pairs={{0,2},{1,3},{2,0},{3,1}} | collective-permute-start | bytes 49160 | tf_op jit(solution)/shard_map/ppermute | solution.py:475
  7.1 11.0 %collective-permute-start.4 = (f32[16,256]{1,0:T(8,128)S(1)}, f32[16,256]{1,0:T(8,128)S(1)}, u32[]{:S(2)}, u32[]{:S(2)}) collective-permute-start(f32[16,256]{1,0:T(8,128)S(1)} %get-tuple-element.62), channel_id=1, source_target_pairs={{2,3},{3,2},{4,5},{5,4},{6,7},{7,6},{8,9},{9,8},{10,11},{11,10},{1... | collective-permute-start | bytes 49160 | tf_op jit(solution)/shard_map/ppermute | solution.py:481
  7.8 10.3 %collective-permute-start.3 = (f32[16,256]{1,0:T(8,128)S(1)}, f32[16,256]{1,0:T(8,128)S(1)}, u32[]{:S(2)}, u32[]{:S(2)}) collective-permute-start(f32[16,256]{1,0:T(8,128)S(1)} %get-tuple-element.62), channel_id=1, source_target_pairs={{0,1},{1,0}} | collective-permute-start | bytes 49160 | tf_op jit(solution)/shard_map/ppermute | solution.py:477
  12.2 5.9 %collective-permute-start.2 = (f32[16,256]{1,0:T(8,128)S(1)}, f32[16,256]{1,0:T(8,128)S(1)}, u32[]{:S(2)}, u32[]{:S(2)}) collective-permute-start(f32[16,256]{1,0:T(8,128)S(1)} %get-tuple-element.61), channel_id=1, source_target_pairs={{2,4},{3,5},{4,2},{5,3},{6,8},{7,9},{8,6},{9,7},{10,12},{11,13},{1... | collective-permute-start | bytes 49160 | tf_op jit(solution)/shard_map/ppermute | solution.py:478
  21.3 11.6 %collective-permute-start.6 = (f32[16,256]{1,0:T(8,128)S(1)}, f32[16,256]{1,0:T(8,128)S(1)}, u32[]{:S(2)}, u32[]{:S(2)}) collective-permute-start(f32[16,256]{1,0:T(8,128)S(1)} %get-tuple-element.74), channel_id=1, source_target_pairs={{4,6},{5,7},{6,4},{7,5},{8,10},{9,11},{10,8},{11,9},{12,14},{13,15... | collective-permute-start | bytes 49160 | tf_op jit(solution)/shard_map/ppermute | solution.py:479
  22.0 10.9 %collective-permute-start.5 = (f32[16,256]{1,0:T(8,128)S(1)}, f32[16,256]{1,0:T(8,128)S(1)}, u32[]{:S(2)}, u32[]{:S(2)}) collective-permute-start(f32[16,256]{1,0:T(8,128)S(1)} %get-tuple-element.74), channel_id=1, source_target_pairs={{0,2},{1,3},{2,0},{3,1}} | collective-permute-start | bytes 49160 | tf_op jit(solution)/shard_map/ppermute | solution.py:475
  23.9 9.0 %collective-permute-start.9 = (f32[16,256]{1,0:T(8,128)S(1)}, f32[16,256]{1,0:T(8,128)S(1)}, u32[]{:S(2)}, u32[]{:S(2)}) collective-permute-start(f32[16,256]{1,0:T(8,128)S(1)} %get-tuple-element.76), channel_id=1, source_target_pairs={{2,3},{3,2},{4,5},{5,4},{6,7},{7,6},{8,9},{9,8},{10,11},{11,10},{1... | collective-permute-start | bytes 49160 | tf_op jit(solution)/shard_map/ppermute | solution.py:481
  24.6 8.4 %collective-permute-start.8 = (f32[16,256]{1,0:T(8,128)S(1)}, f32[16,256]{1,0:T(8,128)S(1)}, u32[]{:S(2)}, u32[]{:S(2)}) collective-permute-start(f32[16,256]{1,0:T(8,128)S(1)} %get-tuple-element.76), channel_id=1, source_target_pairs={{0,1},{1,0}} | collective-permute-start | bytes 49160 | tf_op jit(solution)/shard_map/ppermute | solution.py:477
  27.0 5.9 %collective-permute-start.7 = (f32[16,256]{1,0:T(8,128)S(1)}, f32[16,256]{1,0:T(8,128)S(1)}, u32[]{:S(2)}, u32[]{:S(2)}) collective-permute-start(f32[16,256]{1,0:T(8,128)S(1)} %get-tuple-element.75), channel_id=1, source_target_pairs={{2,4},{3,5},{4,2},{5,3},{6,8},{7,9},{8,6},{9,7},{10,12},{11,13},{1... | collective-permute-start | bytes 49160 | tf_op jit(solution)/shard_map/ppermute | solution.py:478
